TPU v7x, 512 devices: a whole 4x8x8 slice. The times are simulated.
512 devices in a mesh: dp: 64 (over z, y_hi, core), sub: 8 (over y_lo, x).
Axes of the slice: x: 4, y: 8 (y_hi: 4, y_lo: 2; y = y_hi * 2 + y_lo), z: 8, core: 2. Of those that a mesh axis runs over, the one named last changes fastest.
Arguments:
- activations: bfloat16 [1024, 14, 14, 384], P(('dp', 'sub')), may hold values from -6 to 6
- cotangent: bfloat16 [1024, 14, 14, 384], P(('dp', 'sub')), may hold values from -0.29882812 to 0.29882812
- kernel: bfloat16 [384, 1152], replicated, may hold values from -0.1875 to 0.1875
- channel_gain: float32 [384], replicated, may hold values from 0.5 to 4
- master_flat: float32 [442368], P(('dp', 'sub')), may hold values from -6 to 6
- moment_mean: float32 [442368], P(('dp', 'sub')), may hold values from -9.408 to 9.408
- moment_square: float32 [442368], P(('dp', 'sub')), may hold values from 0.0401408 to 1.00352
Outputs:
- input_grad: bfloat16 [1024, 14, 14, 384], P(('dp', 'sub'))
- master_next: float32 [442368], P(('dp', 'sub'))
- mean_next: float32 [442368], P(('dp', 'sub'))
- square_next: float32 [442368], P(('dp', 'sub'))
- kernel_next: bfloat16 [384, 1152], replicated
All inputs are finite; a program needn't handle non-finite values.
Results may differ from a plain program's by a relative error of at most 0.006.
Values may be sent and summed in bfloat16 or wider, within the bound.
No kernel may reach another device: no remote copies, remote signals or barrier semaphores. Data moves between devices by JAX's collectives and lax.ppermute only.
A program may use at most 64 MiB of HBM per device.

v0:
```python
import jax
import jax.numpy as jnp
from jax import lax
from jax.sharding import PartitionSpec as P

CMID = 384
CG = 128
ADAM_STEP = 10
GROUPS = 3
FAN = 1152


HALF_ROOT = 0.7071067811865476
INV_ROOT_TAU = 0.3989422804014327


def gelu_slope(values):
    return (
        0.5 * (1.0 + lax.erf(values * HALF_ROOT))
        + values * jnp.exp(-0.5 * values * values) * INV_ROOT_TAU
    )


def forward(images, kernel_taps):
    batch, side = (images.shape[0], images.shape[1])
    padded = jnp.pad(images, ((0, 0), (1, 1), (1, 1), (0, 0))).reshape(
        batch, side + 2, side + 2, GROUPS, CG
    )
    total = jnp.zeros((batch, side, side, GROUPS, CG), jnp.float32)
    for tap_index in range(9):
        row_off, col_off = (tap_index // 3, tap_index % 3)
        window = padded[:, row_off : row_off + side, col_off : col_off + side]
        total = total + jnp.einsum(
            "bhwgc,gdc->bhwgd",
            window,
            kernel_taps[:, :, tap_index, :],
            preferred_element_type=jnp.float32,
        )
    return total.reshape(batch, side, side, GROUPS * CG)


def input_back(pre_grad, kernel_taps):
    batch, side = (pre_grad.shape[0], pre_grad.shape[1])
    padded = jnp.pad(pre_grad, ((0, 0), (1, 1), (1, 1), (0, 0))).reshape(
        batch, side + 2, side + 2, GROUPS, CG
    )
    total = jnp.zeros((batch, side, side, GROUPS, CG), jnp.float32)
    for tap_index in range(9):
        row_off, col_off = (tap_index // 3, tap_index % 3)
        window = padded[:, 2 - row_off : 2 - row_off + side, 2 - col_off : 2 - col_off + side]
        total = total + jnp.einsum(
            "bhwgd,gdc->bhwgc",
            window,
            kernel_taps[:, :, tap_index, :],
            preferred_element_type=jnp.float32,
        )
    return total.reshape(batch, side, side, GROUPS * CG)


def kernel_back(images, pre_grad):
    batch, side = (images.shape[0], images.shape[1])
    padded = jnp.pad(images, ((0, 0), (1, 1), (1, 1), (0, 0))).reshape(
        batch, side + 2, side + 2, GROUPS, CG
    )
    upstream = pre_grad.reshape(batch, side, side, GROUPS, CG)
    terms = []
    for tap_index in range(9):
        row_off, col_off = (tap_index // 3, tap_index % 3)
        window = padded[:, row_off : row_off + side, col_off : col_off + side]
        terms.append(
            jnp.einsum("bhwgc,bhwgd->gdc", window, upstream, preferred_element_type=jnp.float32)
        )
    return jnp.stack(terms, axis=2).reshape(GROUPS * CG * 9 * CG)


def channel_scale(sum_plain, sum_square, channel_gain):
    chan_mean = sum_plain / FAN
    chan_var = sum_square / FAN - chan_mean * chan_mean
    return (chan_mean, channel_gain / jnp.sqrt(FAN * chan_var + 0.0001))


def on_device(
    activations, cotangent, kernel, channel_gain, master_flat, moment_mean, moment_square
):
    kernel_taps = kernel.reshape(GROUPS, CG, 9, CG)
    preact = forward(activations, kernel_taps)
    pre_grad = (cotangent.astype(jnp.float32) * gelu_slope(preact)).astype(jnp.bfloat16)
    grad_full = kernel_back(activations, pre_grad)
    grad_shard = lax.psum_scatter(grad_full, ("dp", "sub"), scatter_dimension=0, tiled=True)
    input_grad = input_back(pre_grad, kernel_taps).astype(jnp.bfloat16)
    mean_next = 0.9 * moment_mean + 0.1 * grad_shard
    square_next = 0.999 * moment_square + 0.001 * grad_shard * grad_shard
    fix_mean = 1.0 - 0.9**ADAM_STEP
    fix_square = 1.0 - 0.999**ADAM_STEP
    update = mean_next / fix_mean / (jnp.sqrt(square_next / fix_square) + 1e-08)
    master_next = master_flat - 0.02 * update
    shard_len = master_next.shape[0]
    shard_start = lax.axis_index(("dp", "sub")) * shard_len
    first_chan = shard_start // FAN
    chan_span = shard_len // FAN + 2
    offsets = shard_start + jnp.arange(shard_len, dtype=jnp.int32)
    local_chan = offsets // FAN - first_chan
    onehot = (local_chan[:, None] == jnp.arange(chan_span, dtype=jnp.int32)[None, :]).astype(
        jnp.float32
    )
    highest = lax.Precision.HIGHEST
    plain_part = jnp.dot(master_next, onehot, precision=highest)
    square_part = jnp.dot(master_next * master_next, onehot, precision=highest)
    empty = jnp.zeros((CMID + chan_span,), jnp.float32)
    plain_full = lax.dynamic_update_slice(empty, plain_part, (first_chan,))[:CMID]
    square_full = lax.dynamic_update_slice(empty, square_part, (first_chan,))[:CMID]
    sum_plain, sum_square = lax.psum((plain_full, square_full), ("dp", "sub"))
    chan_mean, chan_scale = channel_scale(sum_plain, sum_square, channel_gain)
    mean_window = lax.dynamic_slice(
        jnp.concatenate([chan_mean, empty[:chan_span]]), (first_chan,), (chan_span,)
    )
    scale_window = lax.dynamic_slice(
        jnp.concatenate([chan_scale, empty[:chan_span]]), (first_chan,), (chan_span,)
    )
    entry_mean = jnp.dot(onehot, mean_window, precision=highest)
    entry_scale = jnp.dot(onehot, scale_window, precision=highest)
    standard_shard = ((master_next - entry_mean) * entry_scale).astype(jnp.bfloat16)
    kernel_next = lax.all_gather(standard_shard, ("dp", "sub"), axis=0, tiled=True).reshape(
        CMID, FAN
    )
    return (input_grad, master_next, mean_next, square_next, kernel_next)


def solution(mesh):
    placed = (
        P(("dp", "sub"), None, None, None),
        P(("dp", "sub"), None, None, None),
        P(),
        P(),
        P(("dp", "sub")),
        P(("dp", "sub")),
        P(("dp", "sub")),
    )
    return jax.shard_map(
        on_device,
        mesh=mesh,
        in_specs=placed,
        out_specs=(
            P(("dp", "sub"), None, None, None),
            P(("dp", "sub")),
            P(("dp", "sub")),
            P(("dp", "sub")),
            P(),
        ),
        check_vma=False,
    )
```

profile of v0, /device:TPU:1, one launch (start us, length us, event | category | flops | bytes accessed | tf_op | source)
XLA Modules:
  0.0 697.2 jit_solution(7858080399761789698)
XLA Ops:
  7.2 1.2 pad.10
  8.7 2.0 fusion.73
  10.7 2.3 reshape.83
  13.1 1.9 fusion.71
  15.7 0.7 copy-done.7
  19.2 0.5 reshape.49
  19.8 1.2 fusion.17
  22.3 0.7 copy-done.8
  23.3 0.7 copy-done.6
  24.3 0.7 copy-done.4
  25.3 0.7 copy-done.2
  27.3 1.1 copy.104
  28.4 1.4 reshape.52
  30.7 1.8 fusion.72
  32.8 1.3 convolution_add_fusion.7
  36.2 280.1 %all-reduce.12.cloned.1.call-done = f32[442368]{0:T(1024)} async-done(((f32[442368]{0:T(1024)}), f32[442368]{0:T(1024)}) %all-reduce.12.cloned.1.call-update) | async-done | bytes 1769488
  316.4 1.4 fusion.69
  318.9 96.1 %all-reduce.6 = (f32[384]{0:T(512)S(1)}, f32[384]{0:T(512)S(1)}) all-reduce(f32[384]{0:T(512)S(1)} %bitcast.173, f32[384]{0:T(512)S(1)} %bitcast.172), channel_id=1, replica_groups=mesh['dp'=64,'sub'=8] {'dp','sub'}, use_global_device_ids=true, to_apply=%region_2.3 | all-reduce | flops 768 | bytes 6144 | tf_op jit(solution)/shard_map/psum | solution.py:112
  415.0 0.4 convolution_reduce_fusion.1
  415.5 0.4 convolution_reduce_fusion
  416.3 0.9 copy-done
  418.0 1.0 convert_element_type.23
  419.0 268.5 %all-reduce.10.cloned.1.call-done = bf16[442368]{0:T(1024)(128)(2,1)} async-done(((bf16[442368]{0:T(1024)(128)(2,1)}), bf16[442368]{0:T(1024)(128)(2,1)}) %all-reduce.10.cloned.1.call-update) | async-done | bytes 884752
  687.5 2.9 reshape.53
  (117 shorter events, 12.6 us)
Async XLA Ops:
  7.2 309.2 %all-reduce.12.cloned.1.call-start = ((), (), s32[]{:S(2)}) async-start(), calls=%async_computation.1 | async-start | bytes 3538944
  10.7 6.9 copy-start.1
  13.1 2.0 copy-start.12
  13.1 2.3 copy-start.9
  15.0 1.7 copy-start.24
  15.0 1.7 copy-start.29
  15.0 1.7 copy-start.22
  15.0 2.0 copy-start.20
  15.0 2.7 copy-start.18
  15.0 2.9 copy-start.16
  15.1 3.2 copy-start.26
  15.1 3.2 copy-start.14
  15.1 3.5 copy-start.27
  29.8 657.7 %all-reduce.10.cloned.1.call-start = ((), (), s32[]{:S(2)}) async-start(), calls=%async_computation | async-start | bytes 1769472
  30.7 1.8 copy-start.30
  32.5 1.6 copy-start.25
  32.8 1.6 copy-start.23
  35.3 281.0 %copy-start.33 = (f32[864]{0:T(1024)S(1)}, f32[864]{0:T(1024)}, u32[]{:S(2)}) copy-start(f32[864]{0:T(1024)} %param.11) | copy-start | bytes 10372
  35.3 281.0 %copy-start.34 = (f32[864]{0:T(1024)S(1)}, f32[864]{0:T(1024)}, u32[]{:S(2)}) copy-start(f32[864]{0:T(1024)} %param.12) | copy-start | bytes 10372
  35.3 281.0 %copy-start.35 = (f32[864]{0:T(1024)S(1)}, f32[864]{0:T(1024)}, u32[]{:S(2)}) copy-start(f32[864]{0:T(1024)} %param.13) | copy-start | bytes 10372
  35.3 379.7 %copy-start.36 = (f32[384]{0:T(512)S(1)}, f32[384]{0:T(512)}, u32[]{:S(2)}) copy-start(f32[384]{0:T(512)} %param.10) | copy-start | bytes 4612
  36.0 381.2 %copy-start.15 = (bf16[3,128,1,128]{3,2,1,0:T(2,128)(2,1)S(1)}, bf16[3,128,1,128]{3,2,1,0:T(2,128)(2,1)}, u32[]{:S(2)}) copy-start(bf16[3,128,1,128]{3,2,1,0:T(2,128)(2,1)} %copy-done.14) | copy-start | bytes 294916
  317.7 99.8 %copy-start.32 = (f32[864]{0:T(1024)}, f32[864]{0:T(1024)S(1)}, u32[]{:S(2)}) copy-start(f32[864]{0:T(1024)S(1)} %get-tuple-element.8) | copy-start | bytes 10372
  416.0 1.5 copy-start.11
  (15 other events, 16.3 us)
Sparse Core Ops, SparseCore 0:
  30.0 286.3 all-reduce.11
  417.3 270.1 all-reduce.9
where the time goes:
time: 698 us; the launch traced here: 697 us
  waiting for transfers between devices  549 us (79%)
  blocking collectives  96.1 us (14%)
  local copies, waits for them, and re-layouts  24.7 us (4%)
  between operations  14.8 us (2%)
  matrix products  10.2 us (1%)
    unnamed x4, waiting for transfers between devices  549 us
    psum x1, blocking collectives, on_device(): sum_plain, sum_square = lax.psum((plain_full, square_full), ('dp', 'sub'))  96.1 us
  transfers between devices with their start and end apart: 2, of which 2 were waited for; matrix products, arithmetic and copies ran while one was open for 1% of the time, Pallas kernels for 0%

commit v1 on v0

v1 whole, which is shorter than its diff:
```python
import jax
import jax.numpy as jnp
from jax import lax
from jax.experimental import pallas as pl
from jax.experimental.pallas import tpu as pltpu
from jax.sharding import Mesh, PartitionSpec as P

CMID = 384
CG = 128
ADAM_STEP = 10
GROUPS = 3
FAN = 1152
SIDE = 14
SHARD = 864
HALF_ROOT = 0.7071067811865476
INV_ROOT_TAU = 0.3989422804014327
bf16 = jnp.bfloat16
f32 = jnp.float32

AXES = ("z", "yh", "co", "yl", "x")
SIZES = (8, 4, 2, 2, 4)
ZY = ("z", "yh", "yl")
BLOCKS = CMID // 3
USED = 27
ROWS = 32
IMG = 256
OUT = SIDE * 16
VMEM = pl.BlockSpec(memory_space=pltpu.VMEM)
SMEM = pl.BlockSpec(memory_space=pltpu.SMEM)


def gelu_slope(values):
    return (
        0.5 * (1.0 + lax.erf(values * HALF_ROOT))
        + values * jnp.exp(-0.5 * values * values) * INV_ROOT_TAU
    )


def shift_columns(full, shifted):
    shifted[0] = pltpu.roll(full, 1, 0).astype(bf16)
    shifted[1] = full.astype(bf16)
    shifted[2] = pltpu.roll(full, full.shape[0] - 1, 0).astype(bf16)


def window(shifted, cols, row_off, col_off):
    return jnp.concatenate(
        [shifted[col_off, n * IMG + row_off * 16 : n * IMG + row_off * 16 + OUT, cols] for n in range(2)],
        0,
    )


def grads_kernel(x_ref, cot_ref, k_ref, pg_ref, keep_ref, give_ref, xf, xs, cf, taps, blocks):
    me = lax.axis_index("co")
    xf[...] = jnp.zeros_like(xf)
    cf[...] = jnp.zeros_like(cf)
    for n in range(2):
        for h in range(SIDE):
            at = n * IMG + (h + 1) * 16
            xf[at : at + SIDE, :] = x_ref[n, h].astype(f32)
            at = n * OUT + h * 16
            cf[at : at + SIDE, :] = cot_ref[n, h].astype(f32)
    shift_columns(xf[...], xs)
    pg_ref[...] = jnp.zeros_like(pg_ref)
    for g in range(GROUPS):
        cols = slice(g * CG, (g + 1) * CG)
        patches = jnp.concatenate([window(xs, cols, t // 3, t % 3) for t in range(9)], 1)
        pre = lax.dot_general(
            patches, k_ref[cols, :], (((1,), (1,)), ((), ())), preferred_element_type=f32
        )
        pg = (cf[:, cols] * gelu_slope(pre)).astype(bf16)
        for n in range(2):
            pg_ref[n * IMG + 16 : n * IMG + 16 + OUT, cols] = pg[n * OUT : (n + 1) * OUT]
        grad = lax.dot_general(pg, patches, (((0,), (0,)), ((), ())), preferred_element_type=f32)
        for t in range(9):
            taps[t, cols, :] = grad[:, t * CG : (t + 1) * CG]
    for t in range(9):
        for r in range(3):
            blocks[pl.ds(9 * r + t, BLOCKS, ROWS), :] = taps[t, pl.ds(r, BLOCKS, 3), :]
    for s in range(USED, ROWS):
        blocks[pl.ds(s, BLOCKS, ROWS), :] = jnp.zeros((BLOCKS, CG), f32)
    for q in range(32):
        kept = pl.multiple_of((2 * q + me) * 64, 64)
        given = pl.multiple_of((2 * q + 1 - me) * 64, 64)
        keep_ref[q * 64 : (q + 1) * 64, :] = blocks[pl.ds(kept, 64), :].astype(bf16)
        give_ref[q * 64 : (q + 1) * 64, :] = blocks[pl.ds(given, 64), :].astype(bf16)


def input_kernel(pg_ref, k_ref, out_ref, ps):
    shift_columns(pg_ref[...].astype(f32), ps)
    for g in range(GROUPS):
        cols = slice(g * CG, (g + 1) * CG)
        patches = jnp.concatenate([window(ps, cols, 2 - t // 3, 2 - t % 3) for t in range(9)], 1)
        taps = jnp.concatenate([k_ref[cols, t * CG : (t + 1) * CG] for t in range(9)], 0)
        back = jnp.dot(patches, taps, preferred_element_type=f32).astype(bf16)
        for n in range(2):
            for h in range(SIDE):
                at = n * OUT + h * 16
                out_ref[n, h, :, cols] = back[at : at + SIDE]


def reduce_kernel(part_ref, mean_ref, square_ref, master_ref, out_ref):
    total = part_ref[0:ROWS, :].astype(f32)
    for i in range(1, 64):
        total = total + part_ref[i * ROWS : (i + 1) * ROWS, :].astype(f32)
    for i in range(4):
        out_ref[i, 0:32, :] = total
        out_ref[i, 32:40, :] = mean_ref[...]
        out_ref[i, 40:48, :] = square_ref[...]
        out_ref[i, 48:56, :] = master_ref[...]


def adam(moment_mean, moment_square, master, grad):
    mean_next = 0.9 * moment_mean + 0.1 * grad
    square_next = 0.999 * moment_square + 0.001 * grad * grad
    fix_mean = 1.0 - 0.9**ADAM_STEP
    fix_square = 1.0 - 0.999**ADAM_STEP
    update = mean_next / fix_mean / (jnp.sqrt(square_next / fix_square) + 1e-08)
    return mean_next, square_next, master - 0.02 * update


def adam_kernel(in_ref, gain_ref, grad_ref, send_ref, frame):
    lane = lax.broadcasted_iota(jnp.int32, (8, CG), 1)
    frame[...] = jnp.zeros_like(frame)
    for p in range(4):
        base, shift = divmod(p * SHARD, CG)
        for k in range(3):
            rows = in_ref[p, 32 + 8 * k : 40 + 8 * k, :]
            if shift:
                rows = pltpu.roll(rows, shift, 1)
            frame[k, base : base + 8, :] += jnp.where(lane >= shift, rows, 0.0)
            if shift:
                frame[k, base + 1 : base + 9, :] += jnp.where(lane < shift, rows, 0.0)
    grad = (in_ref[0, 0:32, :] + in_ref[1, 0:32, :]) + (in_ref[2, 0:32, :] + in_ref[3, 0:32, :])
    grad_ref[...] = grad
    master = adam(frame[0, 0:32, :], frame[1, 0:32, :], frame[2, 0:32, :], grad)[2]
    row = lax.broadcasted_iota(jnp.int32, (32, CG), 0)
    block = (lax.axis_index("z") * 4 + lax.axis_index("yh")) * 4 + lax.axis_index("co") * 2 + lax.axis_index("yl")
    mean_of = jnp.zeros((32, CG), f32)
    scale_of = jnp.zeros((32, CG), f32)
    for r in range(3):
        mine = (row >= 9 * r) & (row < 9 * r + 9)
        values = jnp.where(mine, master, 0.0)
        mean = jnp.sum(jnp.sum(values, 0, keepdims=True), 1, keepdims=True) / FAN
        square = jnp.sum(jnp.sum(values * values, 0, keepdims=True), 1, keepdims=True) / FAN
        scale = gain_ref[block * 3 + r] / jnp.sqrt(FAN * (square - mean * mean) + 0.0001)
        mean_of = jnp.where(mine, mean, mean_of)
        scale_of = jnp.where(mine, scale, scale_of)
    out = ((master - mean_of) * scale_of).astype(bf16)
    for i in range(64):
        send_ref[i * ROWS : (i + 1) * ROWS, :] = out


def assemble_kernel(own_ref, got_ref, out_ref, blocks, taps):
    me = lax.axis_index("co")
    for q in range(32):
        kept = pl.multiple_of((2 * q + me) * 64, 64)
        given = pl.multiple_of((2 * q + 1 - me) * 64, 64)
        blocks[pl.ds(kept, 64), :] = own_ref[q * 64 : (q + 1) * 64, :].astype(f32)
        blocks[pl.ds(given, 64), :] = got_ref[q * 64 : (q + 1) * 64, :].astype(f32)
    for t in range(9):
        for r in range(3):
            taps[t, pl.ds(r, BLOCKS, 3), :] = blocks[pl.ds(9 * r + t, BLOCKS, ROWS), :]
    for t in range(9):
        out_ref[:, t * CG : (t + 1) * CG] = taps[t].astype(bf16)


def shape(dims, dtype):
    return jax.ShapeDtypeStruct(dims, dtype)


def swap_cores(x):
    return lax.ppermute(x, "co", [(0, 1), (1, 0)])


def exchange(x, axes):
    return lax.all_to_all(x, axes, 0, 0, tiled=True)


def on_device(
    activations, cotangent, kernel, channel_gain, master_flat, moment_mean, moment_square
):
    pre_grad, keep, give = pl.pallas_call(
        grads_kernel,
        out_shape=(
            shape((2 * IMG, CMID), bf16),
            shape((64 * ROWS, CG), bf16),
            shape((64 * ROWS, CG), bf16),
        ),
        in_specs=[VMEM] * 3,
        out_specs=(VMEM,) * 3,
        scratch_shapes=[
            pltpu.VMEM((2 * IMG, CMID), f32),
            pltpu.VMEM((3, 2 * IMG, CMID), bf16),
            pltpu.VMEM((2 * OUT, CMID), f32),
            pltpu.VMEM((9, CMID, CG), f32),
            pltpu.VMEM((BLOCKS * ROWS, CG), f32),
        ],
        name="grads",
    )(activations, cotangent, kernel)
    got = swap_cores(give)
    input_grad = pl.pallas_call(
        input_kernel,
        out_shape=shape((2, SIDE, SIDE, CMID), bf16),
        in_specs=[VMEM] * 2,
        out_specs=VMEM,
        scratch_shapes=[pltpu.VMEM((3, 2 * IMG, CMID), bf16)],
        name="input_grad",
    )(pre_grad, kernel)
    pair = (keep.astype(f32) + got.astype(f32)).astype(bf16)
    parts = exchange(pair.reshape(64, ROWS, CG), ZY)
    padded = [
        jnp.pad(flat, (0, 1024 - SHARD)).reshape(8, CG)
        for flat in (moment_mean, moment_square, master_flat)
    ]
    payload = pl.pallas_call(
        reduce_kernel,
        out_shape=shape((4, 56, CG), f32),
        in_specs=[VMEM] * 4,
        out_specs=VMEM,
        name="reduce",
    )(parts.reshape(64 * ROWS, CG), *padded)
    gathered = exchange(payload, "x")
    grad, send = pl.pallas_call(
        adam_kernel,
        out_shape=(shape((ROWS, CG), f32), shape((64 * ROWS, CG), bf16)),
        in_specs=[VMEM, SMEM],
        out_specs=(VMEM,) * 2,
        scratch_shapes=[pltpu.VMEM((3, 40, CG), f32)],
        name="adam",
    )(gathered, channel_gain)
    own = exchange(send.reshape(64, ROWS, CG), ZY).reshape(64 * ROWS, CG)
    other = swap_cores(own)
    grad_shard = lax.dynamic_slice(
        grad.reshape(ROWS * CG), (lax.axis_index("x") * SHARD,), (SHARD,)
    )
    mean_next, square_next, master_next = adam(
        moment_mean, moment_square, master_flat, grad_shard
    )
    kernel_next = pl.pallas_call(
        assemble_kernel,
        out_shape=shape((CMID, FAN), bf16),
        in_specs=[VMEM] * 2,
        out_specs=VMEM,
        scratch_shapes=[
            pltpu.VMEM((BLOCKS * ROWS, CG), f32),
            pltpu.VMEM((9, CMID, CG), f32),
        ],
        name="assemble",
    )(own, other)
    return (input_grad, master_next, mean_next, square_next, kernel_next)


def solution(mesh):
    fine = Mesh(mesh.devices.reshape(SIZES), AXES)
    images = P(AXES, None, None, None)
    state = P(AXES)
    return jax.shard_map(
        on_device,
        mesh=fine,
        in_specs=(images, images, P(), P(), state, state, state),
        out_specs=(images, state, state, state, P()),
        check_vma=False,
    )
```

time: 698 us -> 105 us (0.15)
  waiting for transfers between devices: 549 us -> 18 us
  blocking collectives: 96.1 us -> 30.7 us
  starting transfers between devices: 0.26 us -> 27.2 us
  local copies, waits for them, and re-layouts: 24.7 us -> 7.4 us
  Pallas kernels: 0 us -> 17 us
  between operations: 14.8 us -> 0.7 us
  matrix products: 10.2 us -> 0 us
    unnamed x4 -> x0, waiting for transfers between devices: 549 us -> none
    psum x1 -> x0, blocking collectives: 96.1 us -> none  [on_device(): sum_plain, sum_square = lax.psum((plain_full, square_full), ('dp', 'sub'))]
    all_to_all x0 -> x2, blocking collectives: none -> 30.7 us  [exchange(): return lax.all_to_all(x, axes, 0, 0, tiled=True)]
    pallas_call x0 -> x5, Pallas kernels: none -> 17 us  [the longest x1 6.41 us: on_device(): pl.pallas_call(grads_kernel, out_shape=(shape((2 * IMG, CMID), bf16), sha...]
    all_to_all x0 -> x1, waiting for transfers between devices: none -> 16.3 us  [exchange(): return lax.all_to_all(x, axes, 0, 0, tiled=True)]
    ppermute x0 -> x2, starting transfers between devices: none -> 16.1 us  [swap_cores(): return lax.ppermute(x, 'co', [(0, 1), (1, 0)])]
    all_to_all x0 -> x1, starting transfers between devices: none -> 11.1 us  [exchange(): return lax.all_to_all(x, axes, 0, 0, tiled=True)]
    dot_general x31 -> x0, matrix products: 10.2 us -> none  [the longest x9 3.27 us: input_back(): jnp.einsum('bhwgd,gdc->bhwgc', window, kernel_taps[:, :, tap_index, :], p...]
  transfers between devices with their start and end apart: 2 -> 3, of which waited for: 2 -> 2; matrix products, arithmetic and copies ran while one was open for 1% -> 4% of each run, Pallas kernels for 0% -> 3%
where the time goes in v1:
time: 105 us; the launch traced here: 104 us
  blocking collectives  30.7 us (29%)
  starting transfers between devices  27.2 us (26%)
  waiting for transfers between devices  18 us (17%)
  Pallas kernels  17 us (16%)
  local copies, waits for them, and re-layouts  7.4 us (7%)
  other arithmetic  3.36 us (3%)
    all_to_all x2, blocking collectives, exchange(): return lax.all_to_all(x, axes, 0, 0, tiled=True)  30.7 us
    all_to_all x1, waiting for transfers between devices, exchange(): return lax.all_to_all(x, axes, 0, 0, tiled=True)  16.3 us
    ppermute x2, starting transfers between devices, swap_cores(): return lax.ppermute(x, 'co', [(0, 1), (1, 0)])  16.1 us
    all_to_all x1, starting transfers between devices, exchange(): return lax.all_to_all(x, axes, 0, 0, tiled=True)  11.1 us
    pallas_call x1, Pallas kernels, on_device(): pl.pallas_call(grads_kernel, out_shape=(shape((2 * IMG, CMID), bf16), sha...  6.41 us
    unnamed x17, local copies, waits for them, and re-layouts  6.2 us
    pallas_call x1, Pallas kernels, on_device(): pl.pallas_call(assemble_kernel, out_shape=shape((CMID, FAN), bf16), in_sp...  3.76 us
    pallas_call x1, Pallas kernels, on_device(): pl.pallas_call(input_kernel, out_shape=shape((2, SIDE, SIDE, CMID), bf16)...  3.02 us
  transfers between devices with their start and end apart: 3, of which 2 were waited for; matrix products, arithmetic and copies ran while one was open for 4% of the time, Pallas kernels for 3%

profile of v1, /device:TPU:1, one launch (start us, length us, event | category | flops | bytes accessed | tf_op | source)
XLA Modules:
  0.0 104.3 jit_solution(16614945340671177151)
XLA Ops:
  0.6 1.8 %copy.12.x_ref = bf16[2,14,14,384]{3,2,1,0:T(8,128)(2,1)} copy(bf16[2,14,14,384]{3,0,2,1:T(2,128)(2,1)} %param.7) | data formatting | bytes 602112 | tf_op args[0]
  2.4 0.8 copy.13.cot_ref
  3.2 6.4 %grads.1 = (bf16[512,384]{1,0:T(8,128)(2,1)}, bf16[2048,128]{1,0:T(8,128)(2,1)}, bf16[2048,128]{1,0:T(8,128)(2,1)}) custom-call(bf16[2,14,14,384]{3,2,1,0:T(8,128)(2,1)} %copy.12.x_ref, bf16[2,14,14,384]{3,2,1,0:T(8,128)(2,1)} %copy.13.cot_ref, bf16[384,1152]{1,0:T(8,128)(2,1)} %k_ref.3), custom_call_target="tpu_custom_call" | custom-call | tf_op jit(solution)/shard_map/grads/pallas_call | solution.py:182
  9.6 8.7 %collective-permute-start = (bf16[2048,128]{1,0:T(8,128)(2,1)}, bf16[2048,128]{1,0:T(8,128)(2,1)S(1)}, u32[]{:S(2)}, u32[]{:S(2)}) collective-permute-start(bf16[2048,128]{1,0:T(8,128)(2,1)} %get-tuple-element.12), channel_id=1, source_target_pairs={{0,8},{8,0},{1,9},{9,1},{2,10},{10,2},{3,11},{11,3},{4,12},{12,4},... | collective-permute-start | bytes 1572872 | tf_op jit(solution)/shard_map/ppermute | solution.py:172
  18.4 1.7 %collective-permute-done = bf16[2048,128]{1,0:T(8,128)(2,1)S(1)} collective-permute-done((bf16[2048,128]{1,0:T(8,128)(2,1)}, bf16[2048,128]{1,0:T(8,128)(2,1)S(1)}, u32[]{:S(2)}, u32[]{:S(2)}) %collective-permute-start) | collective-permute-done | bytes 524320 | tf_op jit(solution)/shard_map/ppermute | solution.py:172
  20.1 2.0 %add_convert_fusion = bf16[2048,128]{1,0:T(8,128)(2,1)} fusion(bf16[2048,128]{1,0:T(8,128)(2,1)S(1)} %collective-permute-done, bf16[2048,128]{1,0:T(8,128)(2,1)} %get-tuple-element.11), kind=kLoop, calls=%fused_computation | loop fusion | flops 1048576 | bytes 1572864 | tf_op jit(solution)/shard_map/convert_element_type | solution.py:209
  22.1 11.1 %all-to-all-start = ((bf16[64,32,128]{2,1,0:T(8,128)(2,1)}), bf16[64,32,128]{2,1,0:T(8,128)(2,1)S(1)}, u32[]{:S(2)}, u32[]{:S(2)}) async-start(bf16[64,32,128]{2,1,0:T(8,128)(2,1)} %bitcast), calls=%async_computation | async-start | bytes 1048576 | tf_op jit(solution)/shard_map/all_to_all | solution.py:176
  33.2 0.0 copy-start.6
  33.2 0.6 pad_bitcast_fusion.2.mean_ref
  33.8 0.1 copy-done.5
  33.9 0.0 copy-done.6
  33.9 0.6 pad_bitcast_fusion
  34.5 16.3 %all-to-all-done = bf16[64,32,128]{2,1,0:T(8,128)(2,1)S(1)} async-done(((bf16[64,32,128]{2,1,0:T(8,128)(2,1)}), bf16[64,32,128]{2,1,0:T(8,128)(2,1)S(1)}, u32[]{:S(2)}, u32[]{:S(2)}) %all-to-all-start) | async-done | bytes 524320 | tf_op jit(solution)/shard_map/all_to_all | solution.py:176
  50.8 0.8 copy-done
  51.6 1.8 %reduce.1 = f32[4,56,128]{2,1,0:T(8,128)} custom-call(bf16[2048,128]{1,0:T(8,128)(2,1)} %bitcast.11, f32[8,128]{1,0:T(8,128)} %pad_bitcast_fusion.2.mean_ref, f32[8,128]{1,0:T(8,128)} %get-tuple-element.24.square_ref, f32[8,128]{1,0:T(8,128)} %get-tuple-element.23.master_ref), custom_call_target="tpu_custom_call" | custom-call | tf_op jit(solution)/shard_map/reduce/pallas_call | solution.py:215
  53.4 8.9 %all_to_all.15.in_ref = f32[4,56,128]{2,1,0:T(8,128)} all-to-all(f32[4,56,128]{2,1,0:T(8,128)} %reduce.1), channel_id=1, replica_groups=mesh['z'=8,'yh'=4,'co'=2,'yl'=2,'x'=4] {'x'}, dimensions={0} | all-to-all | bytes 229376 | tf_op jit(solution)/shard_map/all_to_all | solution.py:176
  62.2 2.0 %adam.1 = (f32[32,128]{1,0:T(8,128)}, bf16[2048,128]{1,0:T(8,128)(2,1)}) custom-call(f32[4,56,128]{2,1,0:T(8,128)} %all_to_all.15.in_ref, f32[384]{0:T(512)} %gain_ref.1), custom_call_target="tpu_custom_call" | custom-call | tf_op jit(solution)/shard_map/adam/pallas_call | solution.py:223
  64.2 21.8 %all_to_all.16 = bf16[64,32,128]{2,1,0:T(8,128)(2,1)S(1)} all-to-all(bf16[64,32,128]{2,1,0:T(8,128)(2,1)} %bitcast.14), channel_id=1, replica_groups=mesh['z'=8,'yh'=4,'co'=2,'yl'=2,'x'=4] {'z','yh','yl'}, dimensions={0} | all-to-all | bytes 1048576 | tf_op jit(solution)/shard_map/all_to_all | solution.py:176
  86.0 7.3 %collective-permute-start.1 = (bf16[2048,128]{1,0:T(8,128)(2,1)S(1)}, bf16[2048,128]{1,0:T(8,128)(2,1)S(1)}, u32[]{:S(2)}, u32[]{:S(2)}) collective-permute-start(bf16[2048,128]{1,0:T(8,128)(2,1)S(1)} %bitcast.12), channel_id=1, source_target_pairs={{0,8},{8,0},{1,9},{9,1},{2,10},{10,2},{3,11},{11,3},{4,12},{12,4},... | collective-permute-start | bytes 1572872 | tf_op jit(solution)/shard_map/ppermute | solution.py:172
  93.4 3.0 %input_grad.1 = bf16[2,14,14,384]{3,2,1,0:T(8,128)(2,1)} custom-call(bf16[512,384]{1,0:T(8,128)(2,1)} %get-tuple-element.10.pg_ref, bf16[384,1152]{1,0:T(8,128)(2,1)} %k_ref.3), custom_call_target="tpu_custom_call" | custom-call | tf_op jit(solution)/shard_map/input_grad/pallas_call | solution.py:201
  96.4 1.9 %copy.14 = bf16[2,14,14,384]{3,0,2,1:T(2,128)(2,1)} copy(bf16[2,14,14,384]{3,2,1,0:T(8,128)(2,1)} %input_grad.1) | data formatting | bytes 602112
  98.3 1.4 %multiply_subtract_fusion = (f32[864]{0:T(1024)}, f32[864]{0:T(1024)}, f32[864]{0:T(1024)}) fusion(f32[864]{0:T(1024)S(1)} %copy-done.5, f32[4096]{0:T(1024)} %bitcast.15, s32[]{:T(128)S(6)} %select_n.3, f32[864]{0:T(1024)S(1)} %copy-done.4, f32[864]{0:T(1024)S(1)} %copy-done.6), kind=kLoop, calls=%fused_computation.3 | loop fusion | flops 11232 | bytes 24196 | tf_op jit(solution)/shard_map/sub | solution.py:118
  99.7 0.8 copy-done.2
  100.5 3.8 %assemble.1 = bf16[384,1152]{1,0:T(8,128)(2,1)} custom-call(bf16[2048,128]{1,0:T(8,128)(2,1)} %bitcast.13, bf16[2048,128]{1,0:T(8,128)(2,1)} %copy-done.2), custom_call_target="tpu_custom_call" | custom-call | tf_op jit(solution)/shard_map/assemble/pallas_call | solution.py:239
  (10 shorter events, 0.0 us)
Async XLA Ops:
  0.6 1.8 %copy-start.3 = (bf16[2,14,14,384]{3,0,2,1:T(2,128)(2,1)S(1)}, bf16[2,14,14,384]{3,0,2,1:T(2,128)(2,1)}, u32[]{:S(2)}) copy-start(bf16[2,14,14,384]{3,0,2,1:T(2,128)(2,1)} %param.8) | copy-start | bytes 903172
  9.6 10.5 %collective-permute-start = (bf16[2048,128]{1,0:T(8,128)(2,1)}, bf16[2048,128]{1,0:T(8,128)(2,1)S(1)}, u32[]{:S(2)}, u32[]{:S(2)}) collective-permute-start(bf16[2048,128]{1,0:T(8,128)(2,1)} %get-tuple-element.12), channel_id=1, source_target_pairs={{0,8},{8,0},{1,9},{9,1},{2,10},{10,2},{3,11},{11,3},{4,12},{12,4},... | collective-permute-start | bytes 1572872 | tf_op jit(solution)/shard_map/ppermute | solution.py:172
  22.1 11.1 %copy-start.4 = (f32[864]{0:T(1024)S(1)}, f32[864]{0:T(1024)}, u32[]{:S(2)}) copy-start(f32[864]{0:T(1024)} %param.12) | copy-start | bytes 10372
  22.1 28.7 %all-to-all-start = ((bf16[64,32,128]{2,1,0:T(8,128)(2,1)}), bf16[64,32,128]{2,1,0:T(8,128)(2,1)S(1)}, u32[]{:S(2)}, u32[]{:S(2)}) async-start(bf16[64,32,128]{2,1,0:T(8,128)(2,1)} %bitcast), calls=%async_computation | async-start | bytes 1048576 | tf_op jit(solution)/shard_map/all_to_all | solution.py:176
  33.2 0.7 copy-start.5
  33.2 0.7 copy-start.6
  50.8 0.8 copy-start
  86.0 10.4 %copy-start.1 = (bf16[64,32,128]{2,1,0:T(8,128)(2,1)}, bf16[64,32,128]{2,1,0:T(8,128)(2,1)S(1)}, u32[]{:S(2)}) copy-start(bf16[64,32,128]{2,1,0:T(8,128)(2,1)S(1)} %all_to_all.16) | copy-start | bytes 1572868
  86.0 13.7 %collective-permute-start.1 = (bf16[2048,128]{1,0:T(8,128)(2,1)S(1)}, bf16[2048,128]{1,0:T(8,128)(2,1)S(1)}, u32[]{:S(2)}, u32[]{:S(2)}) collective-permute-start(bf16[2048,128]{1,0:T(8,128)(2,1)S(1)} %bitcast.12), channel_id=1, source_target_pairs={{0,8},{8,0},{1,9},{9,1},{2,10},{10,2},{3,11},{11,3},{4,12},{12,4},... | collective-permute-start | bytes 1572872 | tf_op jit(solution)/shard_map/ppermute | solution.py:172
  99.7 0.8 copy-start.2

commit v2 on v1

--- a/solution.py
+++ b/solution.py
@@ -27,6 +27,10 @@
 OUT = SIDE * 16
 VMEM = pl.BlockSpec(memory_space=pltpu.VMEM)
 SMEM = pl.BlockSpec(memory_space=pltpu.SMEM)
+
+
+def grant(mib):
+    return pltpu.CompilerParams(vmem_limit_bytes=mib * 2**20)
 
 
 def gelu_slope(values):
@@ -195,6 +199,7 @@
             pltpu.VMEM((9, CMID, CG), f32),
             pltpu.VMEM((BLOCKS * ROWS, CG), f32),
         ],
+        compiler_params=grant(20),
         name="grads",
     )(activations, cotangent, kernel)
     got = swap_cores(give)
@@ -204,10 +209,12 @@
         in_specs=[VMEM] * 2,
         out_specs=VMEM,
         scratch_shapes=[pltpu.VMEM((3, 2 * IMG, CMID), bf16)],
+        compiler_params=grant(12),
         name="input_grad",
     )(pre_grad, kernel)
     pair = (keep.astype(f32) + got.astype(f32)).astype(bf16)
     parts = exchange(pair.reshape(64, ROWS, CG), ZY)
+    parts, input_grad = lax.optimization_barrier((parts, input_grad))
     padded = [
         jnp.pad(flat, (0, 1024 - SHARD)).reshape(8, CG)
         for flat in (moment_mean, moment_square, master_flat)
@@ -217,6 +224,7 @@
         out_shape=shape((4, 56, CG), f32),
         in_specs=[VMEM] * 4,
         out_specs=VMEM,
+        compiler_params=grant(4),
         name="reduce",
     )(parts.reshape(64 * ROWS, CG), *padded)
     gathered = exchange(payload, "x")
@@ -226,6 +234,7 @@
         in_specs=[VMEM, SMEM],
         out_specs=(VMEM,) * 2,
         scratch_shapes=[pltpu.VMEM((3, 40, CG), f32)],
+        compiler_params=grant(4),
         name="adam",
     )(gathered, channel_gain)
     own = exchange(send.reshape(64, ROWS, CG), ZY).reshape(64 * ROWS, CG)
@@ -245,6 +254,7 @@
             pltpu.VMEM((BLOCKS * ROWS, CG), f32),
             pltpu.VMEM((9, CMID, CG), f32),
         ],
+        compiler_params=grant(10),
         name="assemble",
     )(own, other)
     return (input_grad, master_next, mean_next, square_next, kernel_next)

time: 105 us -> 88.9 us (0.85)
  Pallas kernels: 17 us -> 8.56 us
  local copies, waits for them, and re-layouts: 7.4 us -> 2.97 us
  other arithmetic: 3.36 us -> 1.62 us
    unnamed x17 -> x15, local copies, waits for them, and re-layouts: 6.2 us -> 2.96 us
    pallas_call x1, Pallas kernels: 6.41 us -> 4.07 us  [on_device(): pl.pallas_call(grads_kernel, out_shape=(shape((2 * IMG, CMID), bf16), sha...]
    pallas_call x1, Pallas kernels: 3.02 us -> 0.99 us  [on_device(): pl.pallas_call(input_kernel, out_shape=shape((2, SIDE, SIDE, CMID), bf16)...]
    pallas_call x1, Pallas kernels: 1.81 us -> 0.1 us  [on_device(): pl.pallas_call(reduce_kernel, out_shape=shape((4, 56, CG), f32), in_specs...]
    pallas_call x1, Pallas kernels: 3.76 us -> 2.56 us  [on_device(): pl.pallas_call(assemble_kernel, out_shape=shape((CMID, FAN), bf16), in_sp...]
    reshape x2, local copies, waits for them, and re-layouts: 1.19 us -> 0.01 us  [on_device(): jnp.pad(flat, (0, 1024 - SHARD)).reshape(8, CG)]
    pallas_call x1, Pallas kernels: 1.97 us -> 0.83 us  [on_device(): pl.pallas_call(adam_kernel, out_shape=(shape((ROWS, CG), f32), shape((64...]
  transfers between devices with their start and end apart: 3 -> 3, of which waited for: 2 -> 2; matrix products, arithmetic and copies ran while one was open for 4% -> 2% of each run, Pallas kernels for 3% -> 1%
where the time goes in v2:
time: 88.9 us; the launch traced here: 88.5 us
  blocking collectives  30.2 us (34%)
  starting transfers between devices  27 us (30%)
  waiting for transfers between devices  17.4 us (20%)
  Pallas kernels  8.56 us (10%)
  local copies, waits for them, and re-layouts  2.97 us (3%)
  other arithmetic  1.62 us (2%)
    all_to_all x2, blocking collectives, exchange(): return lax.all_to_all(x, axes, 0, 0, tiled=True)  30.2 us
    ppermute x2, starting transfers between devices, swap_cores(): return lax.ppermute(x, 'co', [(0, 1), (1, 0)])  16.1 us
    all_to_all x1, waiting for transfers between devices, exchange(): return lax.all_to_all(x, axes, 0, 0, tiled=True)  15.9 us
    all_to_all x1, starting transfers between devices, exchange(): return lax.all_to_all(x, axes, 0, 0, tiled=True)  11 us
    pallas_call x1, Pallas kernels, on_device(): pl.pallas_call(grads_kernel, out_shape=(shape((2 * IMG, CMID), bf16), sha...  4.07 us
    unnamed x15, local copies, waits for them, and re-layouts  2.96 us
    pallas_call x1, Pallas kernels, on_device(): pl.pallas_call(assemble_kernel, out_shape=shape((CMID, FAN), bf16), in_sp...  2.56 us
  transfers between devices with their start and end apart: 3, of which 2 were waited for; matrix products, arithmetic and copies ran while one was open for 2% of the time, Pallas kernels for 1%

profile of v2, /device:TPU:1, one launch (start us, length us, event | category | flops | bytes accessed | tf_op | source)
XLA Modules:
  0.0 88.5 jit_solution(7000674955677814619)
XLA Ops:
  0.6 0.0 copy-start.2
  0.7 1.1 %copy.12.x_ref = bf16[2,14,14,384]{3,2,1,0:T(8,128)(2,1)S(1)} copy(bf16[2,14,14,384]{3,0,2,1:T(2,128)(2,1)} %param.7) | data formatting | bytes 602112 | tf_op args[0]
  1.8 0.2 copy-done
  2.0 4.1 %grads.1 = (bf16[512,384]{1,0:T(8,128)(2,1)S(1)}, bf16[2048,128]{1,0:T(8,128)(2,1)S(1)}, bf16[2048,128]{1,0:T(8,128)(2,1)S(1)}) custom-call(bf16[2,14,14,384]{3,2,1,0:T(8,128)(2,1)S(1)} %copy.12.x_ref, bf16[2,14,14,384]{3,2,1,0:T(8,128)(2,1)S(1)} %copy.13.cot_ref, bf16[384,1152]{1,0:T(8,128)(2,1)S(1)} %copy-done), custom_call_target="tpu_custom_call" | custom-call | tf_op jit(solution)/shard_map/grads/pallas_call | solution.py:186
  6.1 8.7 %collective-permute-start = (bf16[2048,128]{1,0:T(8,128)(2,1)S(1)}, bf16[2048,128]{1,0:T(8,128)(2,1)S(1)}, u32[]{:S(2)}, u32[]{:S(2)}) collective-permute-start(bf16[2048,128]{1,0:T(8,128)(2,1)S(1)} %get-tuple-element.13), channel_id=1, source_target_pairs={{0,8},{8,0},{1,9},{9,1},{2,10},{10,2},{3,11},{11,3},{4,12},{12,4},... | collective-permute-start | bytes 1572872 | tf_op jit(solution)/shard_map/ppermute | solution.py:176
  14.8 1.5 %collective-permute-done = bf16[2048,128]{1,0:T(8,128)(2,1)S(1)} collective-permute-done((bf16[2048,128]{1,0:T(8,128)(2,1)S(1)}, bf16[2048,128]{1,0:T(8,128)(2,1)S(1)}, u32[]{:S(2)}, u32[]{:S(2)}) %collective-permute-start) | collective-permute-done | bytes 524320 | tf_op jit(solution)/shard_map/ppermute | solution.py:176
  16.3 0.9 %add_convert_fusion = bf16[2048,128]{1,0:T(8,128)(2,1)} fusion(bf16[2048,128]{1,0:T(8,128)(2,1)S(1)} %collective-permute-done, bf16[2048,128]{1,0:T(8,128)(2,1)S(1)} %get-tuple-element.12), kind=kLoop, calls=%fused_computation | loop fusion | flops 1048576 | bytes 1572864 | tf_op jit(solution)/shard_map/convert_element_type | solution.py:215
  17.3 11.0 %all-to-all-start = ((bf16[64,32,128]{2,1,0:T(8,128)(2,1)}), bf16[64,32,128]{2,1,0:T(8,128)(2,1)S(1)}, u32[]{:S(2)}, u32[]{:S(2)}) async-start(bf16[64,32,128]{2,1,0:T(8,128)(2,1)} %bitcast), calls=%async_computation | async-start | bytes 1048576 | tf_op jit(solution)/shard_map/all_to_all | solution.py:180
  28.2 0.0 copy-start.3
  28.3 1.0 %input_grad.1 = bf16[2,14,14,384]{3,2,1,0:T(8,128)(2,1)S(1)} custom-call(bf16[512,384]{1,0:T(8,128)(2,1)S(1)} %get-tuple-element.14.pg_ref, bf16[384,1152]{1,0:T(8,128)(2,1)S(1)} %copy-done), custom_call_target="tpu_custom_call" | custom-call | tf_op jit(solution)/shard_map/input_grad/pallas_call | solution.py:206
  29.3 0.0 copy-start.4
  29.3 0.0 copy-start.5
  29.3 0.7 copy-done.4
  30.0 0.0 copy-done.5
  30.0 15.9 %all-to-all-done = bf16[64,32,128]{2,1,0:T(8,128)(2,1)S(1)} async-done(((bf16[64,32,128]{2,1,0:T(8,128)(2,1)}), bf16[64,32,128]{2,1,0:T(8,128)(2,1)S(1)}, u32[]{:S(2)}, u32[]{:S(2)}) %all-to-all-start) | async-done | bytes 524320 | tf_op jit(solution)/shard_map/all_to_all | solution.py:180
  45.8 0.1 reduce.1
  45.9 8.6 %all_to_all.15.in_ref = f32[4,56,128]{2,1,0:T(8,128)S(1)} all-to-all(f32[4,56,128]{2,1,0:T(8,128)S(1)} %reduce.1), channel_id=1, replica_groups=mesh['z'=8,'yh'=4,'co'=2,'yl'=2,'x'=4] {'x'}, dimensions={0} | all-to-all | bytes 229376 | tf_op jit(solution)/shard_map/all_to_all | solution.py:180
  54.5 0.8 adam.1
  55.3 21.6 %all_to_all.16 = bf16[64,32,128]{2,1,0:T(8,128)(2,1)S(1)} all-to-all(bf16[64,32,128]{2,1,0:T(8,128)(2,1)S(1)} %bitcast.14), channel_id=1, replica_groups=mesh['z'=8,'yh'=4,'co'=2,'yl'=2,'x'=4] {'z','yh','yl'}, dimensions={0} | all-to-all | bytes 1048576 | tf_op jit(solution)/shard_map/all_to_all | solution.py:180
  77.0 7.3 %collective-permute-start.1 = (bf16[2048,128]{1,0:T(8,128)(2,1)S(1)}, bf16[2048,128]{1,0:T(8,128)(2,1)S(1)}, u32[]{:S(2)}, u32[]{:S(2)}) collective-permute-start(bf16[2048,128]{1,0:T(8,128)(2,1)S(1)} %bitcast.12), channel_id=1, source_target_pairs={{0,8},{8,0},{1,9},{9,1},{2,10},{10,2},{3,11},{11,3},{4,12},{12,4},... | collective-permute-start | bytes 1572872 | tf_op jit(solution)/shard_map/ppermute | solution.py:176
  84.3 0.9 %copy.14 = bf16[2,14,14,384]{3,0,2,1:T(2,128)(2,1)} copy(bf16[2,14,14,384]{3,2,1,0:T(8,128)(2,1)S(1)} %input_grad.1) | data formatting | bytes 602112
  85.3 0.7 multiply_subtract_fusion
  85.9 0.0 collective-permute-done.1.got_ref
  85.9 2.6 %assemble.1 = bf16[384,1152]{1,0:T(8,128)(2,1)} custom-call(bf16[2048,128]{1,0:T(8,128)(2,1)S(1)} %bitcast.13, bf16[2048,128]{1,0:T(8,128)(2,1)S(1)} %collective-permute-done.1.got_ref), custom_call_target="tpu_custom_call" | custom-call | tf_op jit(solution)/shard_map/assemble/pallas_call | solution.py:248
  (8 shorter events, 0.1 us)
Async XLA Ops:
  0.6 1.1 %copy-start.2 = (bf16[2,14,14,384]{3,0,2,1:T(2,128)(2,1)S(1)}, bf16[2,14,14,384]{3,0,2,1:T(2,128)(2,1)}, u32[]{:S(2)}) copy-start(bf16[2,14,14,384]{3,0,2,1:T(2,128)(2,1)} %param.8) | copy-start | bytes 903172
  0.6 1.3 %copy-start = (bf16[384,1152]{1,0:T(8,128)(2,1)S(1)}, bf16[384,1152]{1,0:T(8,128)(2,1)}, u32[]{:S(2)}) copy-start(bf16[384,1152]{1,0:T(8,128)(2,1)} %k_ref.3) | copy-start | bytes 2654212
  6.1 10.3 %collective-permute-start = (bf16[2048,128]{1,0:T(8,128)(2,1)S(1)}, bf16[2048,128]{1,0:T(8,128)(2,1)S(1)}, u32[]{:S(2)}, u32[]{:S(2)}) collective-permute-start(bf16[2048,128]{1,0:T(8,128)(2,1)S(1)} %get-tuple-element.13), channel_id=1, source_target_pairs={{0,8},{8,0},{1,9},{9,1},{2,10},{10,2},{3,11},{11,3},{4,12},{12,4},... | collective-permute-start | bytes 1572872 | tf_op jit(solution)/shard_map/ppermute | solution.py:176
  17.3 28.6 %all-to-all-start = ((bf16[64,32,128]{2,1,0:T(8,128)(2,1)}), bf16[64,32,128]{2,1,0:T(8,128)(2,1)S(1)}, u32[]{:S(2)}, u32[]{:S(2)}) async-start(bf16[64,32,128]{2,1,0:T(8,128)(2,1)} %bitcast), calls=%async_computation | async-start | bytes 1048576 | tf_op jit(solution)/shard_map/all_to_all | solution.py:180
  28.2 1.0 %copy-start.3 = (f32[864]{0:T(1024)S(1)}, f32[864]{0:T(1024)}, u32[]{:S(2)}) copy-start(f32[864]{0:T(1024)} %param.12) | copy-start | bytes 10372
  29.3 0.7 copy-start.4
  29.3 0.7 copy-start.5
  45.9 8.6 %copy-start.1 = (f32[384]{0:T(512)S(1)}, f32[384]{0:T(512)}, u32[]{:S(2)}) copy-start(f32[384]{0:T(512)} %gain_ref.1) | copy-start | bytes 4612
  77.0 9.0 %collective-permute-start.1 = (bf16[2048,128]{1,0:T(8,128)(2,1)S(1)}, bf16[2048,128]{1,0:T(8,128)(2,1)S(1)}, u32[]{:S(2)}, u32[]{:S(2)}) collective-permute-start(bf16[2048,128]{1,0:T(8,128)(2,1)S(1)} %bitcast.12), channel_id=1, source_target_pairs={{0,8},{8,0},{1,9},{9,1},{2,10},{10,2},{3,11},{11,3},{4,12},{12,4},... | collective-permute-start | bytes 1572872 | tf_op jit(solution)/shard_map/ppermute | solution.py:176

commit v3 on v2

--- a/solution.py
+++ b/solution.py
@@ -108,9 +108,14 @@
         total = total + part_ref[i * ROWS : (i + 1) * ROWS, :].astype(f32)
     for i in range(4):
         out_ref[i, 0:32, :] = total
-        out_ref[i, 32:40, :] = mean_ref[...]
-        out_ref[i, 40:48, :] = square_ref[...]
-        out_ref[i, 48:56, :] = master_ref[...]
+        out_ref[i, 32:56, :] = jnp.zeros((24, CG), f32)
+    for k, ref in enumerate((mean_ref, square_ref, master_ref)):
+        for row in range(7):
+            at = 32 + 8 * k + row
+            some = min(CG, SHARD - row * CG)
+            values = ref[pl.ds(row * CG, some)].reshape(1, some)
+            for i in range(4):
+                out_ref[i, at : at + 1, 0:some] = values
 
 
 def adam(moment_mean, moment_square, master, grad):
@@ -213,12 +218,8 @@
         name="input_grad",
     )(pre_grad, kernel)
     pair = (keep.astype(f32) + got.astype(f32)).astype(bf16)
+    pair, input_grad = lax.optimization_barrier((pair, input_grad))
     parts = exchange(pair.reshape(64, ROWS, CG), ZY)
-    parts, input_grad = lax.optimization_barrier((parts, input_grad))
-    padded = [
-        jnp.pad(flat, (0, 1024 - SHARD)).reshape(8, CG)
-        for flat in (moment_mean, moment_square, master_flat)
-    ]
     payload = pl.pallas_call(
         reduce_kernel,
         out_shape=shape((4, 56, CG), f32),
@@ -226,7 +227,7 @@
         out_specs=VMEM,
         compiler_params=grant(4),
         name="reduce",
-    )(parts.reshape(64 * ROWS, CG), *padded)
+    )(parts.reshape(64 * ROWS, CG), moment_mean, moment_square, master_flat)
     gathered = exchange(payload, "x")
     grad, send = pl.pallas_call(
         adam_kernel,

time: 88.9 us -> 88 us (0.990)
  blocking collectives: 30.2 us -> 58.7 us
  waiting for transfers between devices: 17.4 us -> 0.52 us
  starting transfers between devices: 27 us -> 16.1 us
    all_to_all x2 -> x3, blocking collectives: 30.2 us -> 58.7 us  [exchange(): return lax.all_to_all(x, axes, 0, 0, tiled=True)]
    all_to_all x1 -> x0, waiting for transfers between devices: 15.9 us -> none  [exchange(): return lax.all_to_all(x, axes, 0, 0, tiled=True)]
    all_to_all x1 -> x0, starting transfers between devices: 11 us -> none  [exchange(): return lax.all_to_all(x, axes, 0, 0, tiled=True)]
    ppermute x2, waiting for transfers between devices: 1.52 us -> 0.52 us  [swap_cores(): return lax.ppermute(x, 'co', [(0, 1), (1, 0)])]
  transfers between devices with their start and end apart: 3 -> 2, of which waited for: 2 -> 1; matrix products, arithmetic and copies ran while one was open for 2% -> 2% of each run, Pallas kernels for 1% -> 1%
where the time goes in v3:
time: 88 us; the launch traced here: 87.7 us
  blocking collectives  58.7 us (67%)
  starting transfers between devices  16.1 us (18%)
  Pallas kernels  8.57 us (10%)
  local copies, waits for them, and re-layouts  2.3 us (3%)
    all_to_all x3, blocking collectives, exchange(): return lax.all_to_all(x, axes, 0, 0, tiled=True)  58.7 us
    ppermute x2, starting transfers between devices, swap_cores(): return lax.ppermute(x, 'co', [(0, 1), (1, 0)])  16.1 us
    pallas_call x1, Pallas kernels, on_device(): pl.pallas_call(grads_kernel, out_shape=(shape((2 * IMG, CMID), bf16), sha...  4.08 us
    pallas_call x1, Pallas kernels, on_device(): pl.pallas_call(assemble_kernel, out_shape=shape((CMID, FAN), bf16), in_sp...  2.56 us
    unnamed x15, local copies, waits for them, and re-layouts  2.3 us
  transfers between devices with their start and end apart: 2, of which 1 were waited for; matrix products, arithmetic and copies ran while one was open for 2% of the time, Pallas kernels for 1%

profile of v3, /device:TPU:1, one launch (start us, length us, event | category | flops | bytes accessed | tf_op | source)
XLA Modules:
  0.0 87.7 jit_solution(14815920730048943533)
XLA Ops:
  0.6 0.0 copy-start.5
  0.6 0.0 copy-start
  0.7 1.1 %copy.12.x_ref = bf16[2,14,14,384]{3,2,1,0:T(8,128)(2,1)S(1)} copy(bf16[2,14,14,384]{3,0,2,1:T(2,128)(2,1)} %param.7) | data formatting | bytes 602112 | tf_op args[0]
  1.8 0.2 copy-done
  2.0 4.1 %grads.1 = (bf16[512,384]{1,0:T(8,128)(2,1)S(1)}, bf16[2048,128]{1,0:T(8,128)(2,1)S(1)}, bf16[2048,128]{1,0:T(8,128)(2,1)S(1)}) custom-call(bf16[2,14,14,384]{3,2,1,0:T(8,128)(2,1)S(1)} %copy.12.x_ref, bf16[2,14,14,384]{3,2,1,0:T(8,128)(2,1)S(1)} %copy.13.cot_ref, bf16[384,1152]{1,0:T(8,128)(2,1)S(1)} %copy-done), custom_call_target="tpu_custom_call" | custom-call | tf_op jit(solution)/shard_map/grads/pallas_call | solution.py:191
  6.1 8.7 %collective-permute-start = (bf16[2048,128]{1,0:T(8,128)(2,1)S(1)}, bf16[2048,128]{1,0:T(8,128)(2,1)S(1)}, u32[]{:S(2)}, u32[]{:S(2)}) collective-permute-start(bf16[2048,128]{1,0:T(8,128)(2,1)S(1)} %get-tuple-element.13), channel_id=1, source_target_pairs={{0,8},{8,0},{1,9},{9,1},{2,10},{10,2},{3,11},{11,3},{4,12},{12,4},... | collective-permute-start | bytes 1572872 | tf_op jit(solution)/shard_map/ppermute | solution.py:181
  14.8 1.0 %input_grad.1 = bf16[2,14,14,384]{3,2,1,0:T(8,128)(2,1)S(1)} custom-call(bf16[512,384]{1,0:T(8,128)(2,1)S(1)} %get-tuple-element.14.pg_ref, bf16[384,1152]{1,0:T(8,128)(2,1)S(1)} %copy-done), custom_call_target="tpu_custom_call" | custom-call | tf_op jit(solution)/shard_map/input_grad/pallas_call | solution.py:211
  15.8 0.5 collective-permute-done
  16.3 0.1 add_convert_fusion
  16.5 0.0 copy-start.1
  16.5 0.0 copy-start.2
  16.5 0.0 copy-start.3
  16.5 28.5 %all_to_all.15 = bf16[64,32,128]{2,1,0:T(8,128)(2,1)S(1)} all-to-all(bf16[64,32,128]{2,1,0:T(8,128)(2,1)S(1)} %bitcast.10), channel_id=1, replica_groups=mesh['z'=8,'yh'=4,'co'=2,'yl'=2,'x'=4] {'z','yh','yl'}, dimensions={0} | all-to-all | bytes 1048576 | tf_op jit(solution)/shard_map/all_to_all | solution.py:185
  45.0 0.0 copy-done.1
  45.0 0.1 reduce.1
  45.1 8.6 %all_to_all.16.in_ref = f32[4,56,128]{2,1,0:T(8,128)S(1)} all-to-all(f32[4,56,128]{2,1,0:T(8,128)S(1)} %reduce.1), channel_id=1, replica_groups=mesh['z'=8,'yh'=4,'co'=2,'yl'=2,'x'=4] {'x'}, dimensions={0} | all-to-all | bytes 229376 | tf_op jit(solution)/shard_map/all_to_all | solution.py:185
  53.7 0.0 copy-done.4
  53.7 0.8 adam.1
  54.5 21.6 %all_to_all.17 = bf16[64,32,128]{2,1,0:T(8,128)(2,1)S(1)} all-to-all(bf16[64,32,128]{2,1,0:T(8,128)(2,1)S(1)} %bitcast.8), channel_id=1, replica_groups=mesh['z'=8,'yh'=4,'co'=2,'yl'=2,'x'=4] {'z','yh','yl'}, dimensions={0} | all-to-all | bytes 1048576 | tf_op jit(solution)/shard_map/all_to_all | solution.py:185
  76.2 7.3 %collective-permute-start.1 = (bf16[2048,128]{1,0:T(8,128)(2,1)S(1)}, bf16[2048,128]{1,0:T(8,128)(2,1)S(1)}, u32[]{:S(2)}, u32[]{:S(2)}) collective-permute-start(bf16[2048,128]{1,0:T(8,128)(2,1)S(1)} %bitcast.6), channel_id=1, source_target_pairs={{0,8},{8,0},{1,9},{9,1},{2,10},{10,2},{3,11},{11,3},{4,12},{12,4},... | collective-permute-start | bytes 1572872 | tf_op jit(solution)/shard_map/ppermute | solution.py:181
  83.5 0.9 %copy.14 = bf16[2,14,14,384]{3,0,2,1:T(2,128)(2,1)} copy(bf16[2,14,14,384]{3,2,1,0:T(8,128)(2,1)S(1)} %input_grad.1) | data formatting | bytes 602112
  84.4 0.7 multiply_subtract_fusion
  85.1 0.0 collective-permute-done.1.got_ref
  85.1 2.6 %assemble.1 = bf16[384,1152]{1,0:T(8,128)(2,1)} custom-call(bf16[2048,128]{1,0:T(8,128)(2,1)S(1)} %bitcast.7, bf16[2048,128]{1,0:T(8,128)(2,1)S(1)} %collective-permute-done.1.got_ref), custom_call_target="tpu_custom_call" | custom-call | tf_op jit(solution)/shard_map/assemble/pallas_call | solution.py:249
  (5 shorter events, 0.1 us)
Async XLA Ops:
  0.6 1.1 %copy-start.5 = (bf16[2,14,14,384]{3,0,2,1:T(2,128)(2,1)S(1)}, bf16[2,14,14,384]{3,0,2,1:T(2,128)(2,1)}, u32[]{:S(2)}) copy-start(bf16[2,14,14,384]{3,0,2,1:T(2,128)(2,1)} %param.8) | copy-start | bytes 903172
  0.6 1.3 %copy-start = (bf16[384,1152]{1,0:T(8,128)(2,1)S(1)}, bf16[384,1152]{1,0:T(8,128)(2,1)}, u32[]{:S(2)}) copy-start(bf16[384,1152]{1,0:T(8,128)(2,1)} %k_ref.3) | copy-start | bytes 2654212
  6.1 10.3 %collective-permute-start = (bf16[2048,128]{1,0:T(8,128)(2,1)S(1)}, bf16[2048,128]{1,0:T(8,128)(2,1)S(1)}, u32[]{:S(2)}, u32[]{:S(2)}) collective-permute-start(bf16[2048,128]{1,0:T(8,128)(2,1)S(1)} %get-tuple-element.13), channel_id=1, source_target_pairs={{0,8},{8,0},{1,9},{9,1},{2,10},{10,2},{3,11},{11,3},{4,12},{12,4},... | collective-permute-start | bytes 1572872 | tf_op jit(solution)/shard_map/ppermute | solution.py:181
  16.5 28.5 %copy-start.1 = (f32[864]{0:T(1024)S(1)}, f32[864]{0:T(1024)}, u32[]{:S(2)}) copy-start(f32[864]{0:T(1024)} %master_ref.1) | copy-start | bytes 10372
  16.5 28.5 %copy-start.2 = (f32[864]{0:T(1024)S(1)}, f32[864]{0:T(1024)}, u32[]{:S(2)}) copy-start(f32[864]{0:T(1024)} %mean_ref.1) | copy-start | bytes 10372
  16.5 28.5 %copy-start.3 = (f32[864]{0:T(1024)S(1)}, f32[864]{0:T(1024)}, u32[]{:S(2)}) copy-start(f32[864]{0:T(1024)} %square_ref.1) | copy-start | bytes 10372
  45.1 8.6 %copy-start.4 = (f32[384]{0:T(512)S(1)}, f32[384]{0:T(512)}, u32[]{:S(2)}) copy-start(f32[384]{0:T(512)} %gain_ref.1) | copy-start | bytes 4612
  76.2 9.0 %collective-permute-start.1 = (bf16[2048,128]{1,0:T(8,128)(2,1)S(1)}, bf16[2048,128]{1,0:T(8,128)(2,1)S(1)}, u32[]{:S(2)}, u32[]{:S(2)}) collective-permute-start(bf16[2048,128]{1,0:T(8,128)(2,1)S(1)} %bitcast.6), channel_id=1, source_target_pairs={{0,8},{8,0},{1,9},{9,1},{2,10},{10,2},{3,11},{11,3},{4,12},{12,4},... | collective-permute-start | bytes 1572872 | tf_op jit(solution)/shard_map/ppermute | solution.py:181

commit v4 on v3

--- a/solution.py
+++ b/solution.py
@@ -53,40 +53,61 @@
     )
 
 
+def widen(cells):
+    return jnp.concatenate([cells.astype(f32), jnp.zeros((2, CMID), f32)], 0)
+
+
 def grads_kernel(x_ref, cot_ref, k_ref, pg_ref, keep_ref, give_ref, xf, xs, cf, taps, blocks):
     me = lax.axis_index("co")
-    xf[...] = jnp.zeros_like(xf)
-    cf[...] = jnp.zeros_like(cf)
     for n in range(2):
+        for at in (n * IMG, n * IMG + 240):
+            xf[at : at + 16, :] = jnp.zeros((16, CMID), f32)
+            pg_ref[at : at + 16, :] = jnp.zeros((16, CMID), bf16)
         for h in range(SIDE):
             at = n * IMG + (h + 1) * 16
-            xf[at : at + SIDE, :] = x_ref[n, h].astype(f32)
+            xf[at : at + 16, :] = widen(x_ref[n, h])
             at = n * OUT + h * 16
-            cf[at : at + SIDE, :] = cot_ref[n, h].astype(f32)
+            cf[at : at + 16, :] = widen(cot_ref[n, h])
     shift_columns(xf[...], xs)
-    pg_ref[...] = jnp.zeros_like(pg_ref)
-    for g in range(GROUPS):
+    def group(g):
         cols = slice(g * CG, (g + 1) * CG)
-        patches = jnp.concatenate([window(xs, cols, t // 3, t % 3) for t in range(9)], 1)
-        pre = lax.dot_general(
+        return cols, jnp.concatenate([window(xs, cols, t // 3, t % 3) for t in range(9)], 1)
+
+    def forward(g):
+        cols, patches = group(g)
+        return lax.dot_general(
             patches, k_ref[cols, :], (((1,), (1,)), ((), ())), preferred_element_type=f32
         )
+
+    def slope(g, pre):
+        cols = slice(g * CG, (g + 1) * CG)
         pg = (cf[:, cols] * gelu_slope(pre)).astype(bf16)
         for n in range(2):
             pg_ref[n * IMG + 16 : n * IMG + 16 + OUT, cols] = pg[n * OUT : (n + 1) * OUT]
+        return pg
+
+    def weight(g, pg):
+        cols, patches = group(g)
         grad = lax.dot_general(pg, patches, (((0,), (0,)), ((), ())), preferred_element_type=f32)
         for t in range(9):
             taps[t, cols, :] = grad[:, t * CG : (t + 1) * CG]
+
+    pre = [forward(g) for g in range(GROUPS)]
+    for g in range(GROUPS):
+        weight(g, slope(g, pre[g]))
     for t in range(9):
         for r in range(3):
-            blocks[pl.ds(9 * r + t, BLOCKS, ROWS), :] = taps[t, pl.ds(r, BLOCKS, 3), :]
-    for s in range(USED, ROWS):
-        blocks[pl.ds(s, BLOCKS, ROWS), :] = jnp.zeros((BLOCKS, CG), f32)
-    for q in range(32):
-        kept = pl.multiple_of((2 * q + me) * 64, 64)
-        given = pl.multiple_of((2 * q + 1 - me) * 64, 64)
-        keep_ref[q * 64 : (q + 1) * 64, :] = blocks[pl.ds(kept, 64), :].astype(bf16)
-        give_ref[q * 64 : (q + 1) * 64, :] = blocks[pl.ds(given, 64), :].astype(bf16)
+            blocks[pl.ds(9 * r + t, BLOCKS, USED), :] = taps[t, pl.ds(r, BLOCKS, 3), :]
+    blocks[BLOCKS * USED :, :] = jnp.zeros((8, CG), f32)
+    for core in range(2):
+
+        @pl.when(me == core)
+        def _():
+            for q in range(64):
+                kept = (q // 2 * 4 + 2 * core + q % 2) * USED
+                given = (q // 2 * 4 + 2 - 2 * core + q % 2) * USED
+                keep_ref[q * ROWS : (q + 1) * ROWS, :] = blocks[kept : kept + ROWS, :].astype(bf16)
+                give_ref[q * ROWS : (q + 1) * ROWS, :] = blocks[given : given + ROWS, :].astype(bf16)
 
 
 def input_kernel(pg_ref, k_ref, out_ref, ps):
@@ -161,14 +182,19 @@
 
 def assemble_kernel(own_ref, got_ref, out_ref, blocks, taps):
     me = lax.axis_index("co")
-    for q in range(32):
-        kept = pl.multiple_of((2 * q + me) * 64, 64)
-        given = pl.multiple_of((2 * q + 1 - me) * 64, 64)
-        blocks[pl.ds(kept, 64), :] = own_ref[q * 64 : (q + 1) * 64, :].astype(f32)
-        blocks[pl.ds(given, 64), :] = got_ref[q * 64 : (q + 1) * 64, :].astype(f32)
+    for core in range(2):
+
+        @pl.when(me == core)
+        def _():
+            for q in range(64):
+                kept = (q // 2 * 4 + 2 * core + q % 2) * USED
+                given = (q // 2 * 4 + 2 - 2 * core + q % 2) * USED
+                blocks[kept : kept + USED, :] = own_ref[q * ROWS : q * ROWS + USED, :].astype(f32)
+                blocks[given : given + USED, :] = got_ref[q * ROWS : q * ROWS + USED, :].astype(f32)
+
     for t in range(9):
         for r in range(3):
-            taps[t, pl.ds(r, BLOCKS, 3), :] = blocks[pl.ds(9 * r + t, BLOCKS, ROWS), :]
+            taps[t, pl.ds(r, BLOCKS, 3), :] = blocks[pl.ds(9 * r + t, BLOCKS, USED), :]
     for t in range(9):
         out_ref[:, t * CG : (t + 1) * CG] = taps[t].astype(bf16)
 
@@ -202,7 +228,7 @@
             pltpu.VMEM((3, 2 * IMG, CMID), bf16),
             pltpu.VMEM((2 * OUT, CMID), f32),
             pltpu.VMEM((9, CMID, CG), f32),
-            pltpu.VMEM((BLOCKS * ROWS, CG), f32),
+            pltpu.VMEM((BLOCKS * USED + 8, CG), f32),
         ],
         compiler_params=grant(20),
         name="grads",
@@ -252,7 +278,7 @@
         in_specs=[VMEM] * 2,
         out_specs=VMEM,
         scratch_shapes=[
-            pltpu.VMEM((BLOCKS * ROWS, CG), f32),
+            pltpu.VMEM((BLOCKS * USED + 8, CG), f32),
             pltpu.VMEM((9, CMID, CG), f32),
         ],
         compiler_params=grant(10),

time: 88 us -> 84.6 us (0.961)
  Pallas kernels: 8.57 us -> 5.12 us
    pallas_call x1, Pallas kernels: 4.08 us -> 1.9 us  [on_device(): pl.pallas_call(grads_kernel, out_shape=(shape((2 * IMG, CMID), bf16), sha...]
    pallas_call x1, Pallas kernels: 2.56 us -> 1.3 us  [on_device(): pl.pallas_call(assemble_kernel, out_shape=shape((CMID, FAN), bf16), in_sp...]
where the time goes in v4:
time: 84.6 us; the launch traced here: 84.2 us
  blocking collectives  58.7 us (69%)
  starting transfers between devices  16.1 us (19%)
  Pallas kernels  5.12 us (6%)
  local copies, waits for them, and re-layouts  2.3 us (3%)
    all_to_all x3, blocking collectives, exchange(): return lax.all_to_all(x, axes, 0, 0, tiled=True)  58.7 us
    ppermute x2, starting transfers between devices, swap_cores(): return lax.ppermute(x, 'co', [(0, 1), (1, 0)])  16.1 us
    unnamed x15, local copies, waits for them, and re-layouts  2.3 us
    pallas_call x1, Pallas kernels, on_device(): pl.pallas_call(grads_kernel, out_shape=(shape((2 * IMG, CMID), bf16), sha...  1.9 us
  transfers between devices with their start and end apart: 2, of which 1 were waited for; matrix products, arithmetic and copies ran while one was open for 2% of the time, Pallas kernels for 1%

profile of v4, /device:TPU:1, one launch (start us, length us, event | category | flops | bytes accessed | tf_op | source)
XLA Modules:
  0.0 84.2 jit_solution(16775008413244110836)
XLA Ops:
  0.6 0.0 copy-start.5
  0.6 0.0 copy-start
  0.7 1.1 %copy.12.x_ref = bf16[2,14,14,384]{3,2,1,0:T(8,128)(2,1)S(1)} copy(bf16[2,14,14,384]{3,0,2,1:T(2,128)(2,1)} %param.7) | data formatting | bytes 602112 | tf_op args[0]
  1.8 0.0 copy-done.5
  1.8 0.2 copy-done
  2.0 1.9 %grads.1 = (bf16[512,384]{1,0:T(8,128)(2,1)S(1)}, bf16[2048,128]{1,0:T(8,128)(2,1)S(1)}, bf16[2048,128]{1,0:T(8,128)(2,1)S(1)}) custom-call(bf16[2,14,14,384]{3,2,1,0:T(8,128)(2,1)S(1)} %copy.12.x_ref, bf16[2,14,14,384]{3,2,1,0:T(8,128)(2,1)S(1)} %copy.13.cot_ref, bf16[384,1152]{1,0:T(8,128)(2,1)S(1)} %copy-done), custom_call_target="tpu_custom_call" | custom-call | tf_op jit(solution)/shard_map/grads/pallas_call | solution.py:217
  3.9 8.7 %collective-permute-start = (bf16[2048,128]{1,0:T(8,128)(2,1)S(1)}, bf16[2048,128]{1,0:T(8,128)(2,1)S(1)}, u32[]{:S(2)}, u32[]{:S(2)}) collective-permute-start(bf16[2048,128]{1,0:T(8,128)(2,1)S(1)} %get-tuple-element.13), channel_id=1, source_target_pairs={{0,8},{8,0},{1,9},{9,1},{2,10},{10,2},{3,11},{11,3},{4,12},{12,4},... | collective-permute-start | bytes 1572872 | tf_op jit(solution)/shard_map/ppermute | solution.py:207
  12.6 1.0 %input_grad.1 = bf16[2,14,14,384]{3,2,1,0:T(8,128)(2,1)S(1)} custom-call(bf16[512,384]{1,0:T(8,128)(2,1)S(1)} %get-tuple-element.14.pg_ref, bf16[384,1152]{1,0:T(8,128)(2,1)S(1)} %copy-done), custom_call_target="tpu_custom_call" | custom-call | tf_op jit(solution)/shard_map/input_grad/pallas_call | solution.py:237
  13.6 0.5 collective-permute-done
  14.2 0.1 add_convert_fusion
  14.3 0.0 copy-start.1
  14.3 0.0 copy-start.2
  14.3 0.0 copy-start.3
  14.3 28.5 %all_to_all.15 = bf16[64,32,128]{2,1,0:T(8,128)(2,1)S(1)} all-to-all(bf16[64,32,128]{2,1,0:T(8,128)(2,1)S(1)} %bitcast.10), channel_id=1, replica_groups=mesh['z'=8,'yh'=4,'co'=2,'yl'=2,'x'=4] {'z','yh','yl'}, dimensions={0} | all-to-all | bytes 1048576 | tf_op jit(solution)/shard_map/all_to_all | solution.py:211
  42.8 0.0 copy-done.1
  42.8 0.1 reduce.1
  42.9 8.5 %all_to_all.16.in_ref = f32[4,56,128]{2,1,0:T(8,128)S(1)} all-to-all(f32[4,56,128]{2,1,0:T(8,128)S(1)} %reduce.1), channel_id=1, replica_groups=mesh['z'=8,'yh'=4,'co'=2,'yl'=2,'x'=4] {'x'}, dimensions={0} | all-to-all | bytes 229376 | tf_op jit(solution)/shard_map/all_to_all | solution.py:211
  51.5 0.8 adam.1
  52.3 21.6 %all_to_all.17 = bf16[64,32,128]{2,1,0:T(8,128)(2,1)S(1)} all-to-all(bf16[64,32,128]{2,1,0:T(8,128)(2,1)S(1)} %bitcast.8), channel_id=1, replica_groups=mesh['z'=8,'yh'=4,'co'=2,'yl'=2,'x'=4] {'z','yh','yl'}, dimensions={0} | all-to-all | bytes 1048576 | tf_op jit(solution)/shard_map/all_to_all | solution.py:211
  74.0 7.3 %collective-permute-start.1 = (bf16[2048,128]{1,0:T(8,128)(2,1)S(1)}, bf16[2048,128]{1,0:T(8,128)(2,1)S(1)}, u32[]{:S(2)}, u32[]{:S(2)}) collective-permute-start(bf16[2048,128]{1,0:T(8,128)(2,1)S(1)} %bitcast.6), channel_id=1, source_target_pairs={{0,8},{8,0},{1,9},{9,1},{2,10},{10,2},{3,11},{11,3},{4,12},{12,4},... | collective-permute-start | bytes 1572872 | tf_op jit(solution)/shard_map/ppermute | solution.py:207
  81.3 0.9 %copy.14 = bf16[2,14,14,384]{3,0,2,1:T(2,128)(2,1)} copy(bf16[2,14,14,384]{3,2,1,0:T(8,128)(2,1)S(1)} %input_grad.1) | data formatting | bytes 602112
  82.2 0.7 multiply_subtract_fusion
  82.9 0.0 collective-permute-done.1.got_ref
  82.9 1.3 %assemble.1 = bf16[384,1152]{1,0:T(8,128)(2,1)} custom-call(bf16[2048,128]{1,0:T(8,128)(2,1)S(1)} %bitcast.7, bf16[2048,128]{1,0:T(8,128)(2,1)S(1)} %collective-permute-done.1.got_ref), custom_call_target="tpu_custom_call" | custom-call | tf_op jit(solution)/shard_map/assemble/pallas_call | solution.py:275
  (5 shorter events, 0.1 us)
Async XLA Ops:
  0.6 1.1 %copy-start.5 = (bf16[2,14,14,384]{3,0,2,1:T(2,128)(2,1)S(1)}, bf16[2,14,14,384]{3,0,2,1:T(2,128)(2,1)}, u32[]{:S(2)}) copy-start(bf16[2,14,14,384]{3,0,2,1:T(2,128)(2,1)} %param.8) | copy-start | bytes 903172
  0.6 1.3 %copy-start = (bf16[384,1152]{1,0:T(8,128)(2,1)S(1)}, bf16[384,1152]{1,0:T(8,128)(2,1)}, u32[]{:S(2)}) copy-start(bf16[384,1152]{1,0:T(8,128)(2,1)} %k_ref.3) | copy-start | bytes 2654212
  3.9 10.3 %collective-permute-start = (bf16[2048,128]{1,0:T(8,128)(2,1)S(1)}, bf16[2048,128]{1,0:T(8,128)(2,1)S(1)}, u32[]{:S(2)}, u32[]{:S(2)}) collective-permute-start(bf16[2048,128]{1,0:T(8,128)(2,1)S(1)} %get-tuple-element.13), channel_id=1, source_target_pairs={{0,8},{8,0},{1,9},{9,1},{2,10},{10,2},{3,11},{11,3},{4,12},{12,4},... | collective-permute-start | bytes 1572872 | tf_op jit(solution)/shard_map/ppermute | solution.py:207
  14.3 28.5 %copy-start.1 = (f32[864]{0:T(1024)S(1)}, f32[864]{0:T(1024)}, u32[]{:S(2)}) copy-start(f32[864]{0:T(1024)} %master_ref.1) | copy-start | bytes 10372
  14.3 28.5 %copy-start.2 = (f32[864]{0:T(1024)S(1)}, f32[864]{0:T(1024)}, u32[]{:S(2)}) copy-start(f32[864]{0:T(1024)} %mean_ref.1) | copy-start | bytes 10372
  14.3 28.5 %copy-start.3 = (f32[864]{0:T(1024)S(1)}, f32[864]{0:T(1024)}, u32[]{:S(2)}) copy-start(f32[864]{0:T(1024)} %square_ref.1) | copy-start | bytes 10372
  42.9 8.6 %copy-start.4 = (f32[384]{0:T(512)S(1)}, f32[384]{0:T(512)}, u32[]{:S(2)}) copy-start(f32[384]{0:T(512)} %gain_ref.1) | copy-start | bytes 4612
  74.0 9.0 %collective-permute-start.1 = (bf16[2048,128]{1,0:T(8,128)(2,1)S(1)}, bf16[2048,128]{1,0:T(8,128)(2,1)S(1)}, u32[]{:S(2)}, u32[]{:S(2)}) collective-permute-start(bf16[2048,128]{1,0:T(8,128)(2,1)S(1)} %bitcast.6), channel_id=1, source_target_pairs={{0,8},{8,0},{1,9},{9,1},{2,10},{10,2},{3,11},{11,3},{4,12},{12,4},... | collective-permute-start | bytes 1572872 | tf_op jit(solution)/shard_map/ppermute | solution.py:207

commit v5 on v4

--- a/solution.py
+++ b/solution.py
@@ -23,6 +23,7 @@
 BLOCKS = CMID // 3
 USED = 27
 ROWS = 32
+TILES = 7
 IMG = 256
 OUT = SIDE * 16
 VMEM = pl.BlockSpec(memory_space=pltpu.VMEM)
@@ -106,8 +107,10 @@
             for q in range(64):
                 kept = (q // 2 * 4 + 2 * core + q % 2) * USED
                 given = (q // 2 * 4 + 2 - 2 * core + q % 2) * USED
-                keep_ref[q * ROWS : (q + 1) * ROWS, :] = blocks[kept : kept + ROWS, :].astype(bf16)
-                give_ref[q * ROWS : (q + 1) * ROWS, :] = blocks[given : given + ROWS, :].astype(bf16)
+                for k in range(TILES):
+                    at = 4 * k
+                    keep_ref[q, k] = blocks[kept + at : kept + at + 4, :].astype(bf16)
+                    give_ref[q, k] = blocks[given + at : given + at + 4, :].astype(bf16)
 
 
 def input_kernel(pg_ref, k_ref, out_ref, ps):
@@ -124,12 +127,13 @@
 
 
 def reduce_kernel(part_ref, mean_ref, square_ref, master_ref, out_ref):
-    total = part_ref[0:ROWS, :].astype(f32)
+    total = part_ref[0].astype(f32)
     for i in range(1, 64):
-        total = total + part_ref[i * ROWS : (i + 1) * ROWS, :].astype(f32)
+        total = total + part_ref[i].astype(f32)
     for i in range(4):
-        out_ref[i, 0:32, :] = total
-        out_ref[i, 32:56, :] = jnp.zeros((24, CG), f32)
+        out_ref[i, 24:56, :] = jnp.zeros((32, CG), f32)
+        for k in range(TILES):
+            out_ref[i, 4 * k : 4 * k + 4, :] = total[k]
     for k, ref in enumerate((mean_ref, square_ref, master_ref)):
         for row in range(7):
             at = 32 + 8 * k + row
@@ -175,9 +179,11 @@
         scale = gain_ref[block * 3 + r] / jnp.sqrt(FAN * (square - mean * mean) + 0.0001)
         mean_of = jnp.where(mine, mean, mean_of)
         scale_of = jnp.where(mine, scale, scale_of)
-    out = ((master - mean_of) * scale_of).astype(bf16)
-    for i in range(64):
-        send_ref[i * ROWS : (i + 1) * ROWS, :] = out
+    out = (master - mean_of) * scale_of
+    for k in range(TILES):
+        tile = out[4 * k : 4 * k + 4].astype(bf16)
+        for i in range(64):
+            send_ref[i, k] = tile
 
 
 def assemble_kernel(own_ref, got_ref, out_ref, blocks, taps):
@@ -189,8 +195,10 @@
             for q in range(64):
                 kept = (q // 2 * 4 + 2 * core + q % 2) * USED
                 given = (q // 2 * 4 + 2 - 2 * core + q % 2) * USED
-                blocks[kept : kept + USED, :] = own_ref[q * ROWS : q * ROWS + USED, :].astype(f32)
-                blocks[given : given + USED, :] = got_ref[q * ROWS : q * ROWS + USED, :].astype(f32)
+                for k in range(TILES):
+                    at, some = 4 * k, min(4, USED - 4 * k)
+                    blocks[kept + at : kept + at + some, :] = own_ref[q, k].astype(f32)[:some]
+                    blocks[given + at : given + at + some, :] = got_ref[q, k].astype(f32)[:some]
 
     for t in range(9):
         for r in range(3):
@@ -218,8 +226,8 @@
         grads_kernel,
         out_shape=(
             shape((2 * IMG, CMID), bf16),
-            shape((64 * ROWS, CG), bf16),
-            shape((64 * ROWS, CG), bf16),
+            shape((64, TILES, 4, CG), bf16),
+            shape((64, TILES, 4, CG), bf16),
         ),
         in_specs=[VMEM] * 3,
         out_specs=(VMEM,) * 3,
@@ -245,7 +253,7 @@
     )(pre_grad, kernel)
     pair = (keep.astype(f32) + got.astype(f32)).astype(bf16)
     pair, input_grad = lax.optimization_barrier((pair, input_grad))
-    parts = exchange(pair.reshape(64, ROWS, CG), ZY)
+    parts = exchange(pair, ZY)
     payload = pl.pallas_call(
         reduce_kernel,
         out_shape=shape((4, 56, CG), f32),
@@ -253,18 +261,18 @@
         out_specs=VMEM,
         compiler_params=grant(4),
         name="reduce",
-    )(parts.reshape(64 * ROWS, CG), moment_mean, moment_square, master_flat)
+    )(parts, moment_mean, moment_square, master_flat)
     gathered = exchange(payload, "x")
     grad, send = pl.pallas_call(
         adam_kernel,
-        out_shape=(shape((ROWS, CG), f32), shape((64 * ROWS, CG), bf16)),
+        out_shape=(shape((ROWS, CG), f32), shape((64, TILES, 4, CG), bf16)),
         in_specs=[VMEM, SMEM],
         out_specs=(VMEM,) * 2,
         scratch_shapes=[pltpu.VMEM((3, 40, CG), f32)],
         compiler_params=grant(4),
         name="adam",
     )(gathered, channel_gain)
-    own = exchange(send.reshape(64, ROWS, CG), ZY).reshape(64 * ROWS, CG)
+    own = exchange(send, ZY)
     other = swap_cores(own)
     grad_shard = lax.dynamic_slice(
         grad.reshape(ROWS * CG), (lax.axis_index("x") * SHARD,), (SHARD,)

time: 84.6 us -> 82.2 us (0.972)
  blocking collectives: 58.7 us -> 56.2 us
    all_to_all x3, blocking collectives: 58.7 us -> 56.2 us  [exchange(): return lax.all_to_all(x, axes, 0, 0, tiled=True)]
where the time goes in v5:
time: 82.2 us; the launch traced here: 81.8 us
  blocking collectives  56.2 us (68%)
  starting transfers between devices  15.8 us (19%)
  Pallas kernels  5.49 us (7%)
  local copies, waits for them, and re-layouts  2.3 us (3%)
  other arithmetic  0.93 us (1%)
    all_to_all x3, blocking collectives, exchange(): return lax.all_to_all(x, axes, 0, 0, tiled=True)  56.2 us
    ppermute x2, starting transfers between devices, swap_cores(): return lax.ppermute(x, 'co', [(0, 1), (1, 0)])  15.8 us
    unnamed x15, local copies, waits for them, and re-layouts  2.3 us
    pallas_call x1, Pallas kernels, on_device(): pl.pallas_call(grads_kernel, out_shape=(shape((2 * IMG, CMID), bf16), sha...  2.11 us
  transfers between devices with their start and end apart: 2, of which 1 were waited for; matrix products, arithmetic and copies ran while one was open for 2% of the time, Pallas kernels for 1%

profile of v5, /device:TPU:1, one launch (start us, length us, event | category | flops | bytes accessed | tf_op | source)
XLA Modules:
  0.0 81.8 jit_solution(15209813000642090251)
XLA Ops:
  0.6 0.0 copy-start.5
  0.6 0.0 copy-start
  0.7 1.1 %copy.12.x_ref = bf16[2,14,14,384]{3,2,1,0:T(8,128)(2,1)S(1)} copy(bf16[2,14,14,384]{3,0,2,1:T(2,128)(2,1)} %param.7) | data formatting | bytes 602112 | tf_op args[0]
  1.8 0.0 copy-done.5
  1.8 0.2 copy-done
  2.0 2.1 %grads.1 = (bf16[512,384]{1,0:T(8,128)(2,1)S(1)}, bf16[64,7,4,128]{3,2,1,0:T(4,128)(2,1)S(1)}, bf16[64,7,4,128]{3,2,1,0:T(4,128)(2,1)S(1)}) custom-call(bf16[2,14,14,384]{3,2,1,0:T(8,128)(2,1)S(1)} %copy.12.x_ref, bf16[2,14,14,384]{3,2,1,0:T(8,128)(2,1)S(1)} %copy.13.cot_ref, bf16[384,1152]{1,0:T(8,128)(2,1)S(1)} %copy-done), custom_call_target="tpu_custom_call" | custom-call | tf_op jit(solution)/shard_map/grads/pallas_call | solution.py:225
  4.1 8.7 %collective-permute-start = (bf16[64,7,4,128]{3,2,1,0:T(4,128)(2,1)S(1)}, bf16[64,7,4,128]{3,2,1,0:T(4,128)(2,1)S(1)}, u32[]{:S(2)}, u32[]{:S(2)}) collective-permute-start(bf16[64,7,4,128]{3,2,1,0:T(4,128)(2,1)S(1)} %get-tuple-element.13), channel_id=1, source_target_pairs={{0,8},{8,0},{1,9},{9,1},{2,10},{10,2},{3,11},{11,3},{4,12},{12,4},... | collective-permute-start | bytes 1376264 | tf_op jit(solution)/shard_map/ppermute | solution.py:215
  12.9 1.0 %input_grad.1 = bf16[2,14,14,384]{3,2,1,0:T(8,128)(2,1)S(1)} custom-call(bf16[512,384]{1,0:T(8,128)(2,1)S(1)} %get-tuple-element.14.pg_ref, bf16[384,1152]{1,0:T(8,128)(2,1)S(1)} %copy-done), custom_call_target="tpu_custom_call" | custom-call | tf_op jit(solution)/shard_map/input_grad/pallas_call | solution.py:245
  13.9 0.4 collective-permute-done
  14.3 0.2 add_convert_fusion
  14.5 0.0 copy-start.1
  14.5 0.0 copy-start.2
  14.5 0.0 copy-start.3
  14.6 27.3 %all_to_all.15.part_ref = bf16[64,7,4,128]{3,2,1,0:T(4,128)(2,1)S(1)} all-to-all(bf16[64,7,4,128]{3,2,1,0:T(4,128)(2,1)S(1)} %add_convert_fusion), channel_id=1, replica_groups=mesh['z'=8,'yh'=4,'co'=2,'yl'=2,'x'=4] {'z','yh','yl'}, dimensions={0} | all-to-all | bytes 917504 | tf_op jit(solution)/shard_map/all_to_all | solution.py:219
  41.9 0.2 reduce.1
  42.1 8.5 %all_to_all.16.in_ref = f32[4,56,128]{2,1,0:T(8,128)S(1)} all-to-all(f32[4,56,128]{2,1,0:T(8,128)S(1)} %reduce.1), channel_id=1, replica_groups=mesh['z'=8,'yh'=4,'co'=2,'yl'=2,'x'=4] {'x'}, dimensions={0} | all-to-all | bytes 229376 | tf_op jit(solution)/shard_map/all_to_all | solution.py:219
  50.6 0.0 copy-done.4
  50.6 0.9 %adam.1 = (f32[32,128]{1,0:T(8,128)S(1)}, bf16[64,7,4,128]{3,2,1,0:T(4,128)(2,1)S(1)}) custom-call(f32[4,56,128]{2,1,0:T(8,128)S(1)} %all_to_all.16.in_ref, f32[384]{0:T(512)S(1)} %copy-done.4), custom_call_target="tpu_custom_call" | custom-call | tf_op jit(solution)/shard_map/adam/pallas_call | solution.py:266
  51.5 20.3 %all_to_all.17.own_ref = bf16[64,7,4,128]{3,2,1,0:T(4,128)(2,1)S(1)} all-to-all(bf16[64,7,4,128]{3,2,1,0:T(4,128)(2,1)S(1)} %get-tuple-element.18), channel_id=1, replica_groups=mesh['z'=8,'yh'=4,'co'=2,'yl'=2,'x'=4] {'z','yh','yl'}, dimensions={0} | all-to-all | bytes 917504 | tf_op jit(solution)/shard_map/all_to_all | solution.py:219
  71.8 7.0 %collective-permute-start.1 = (bf16[64,7,4,128]{3,2,1,0:T(4,128)(2,1)S(1)}, bf16[64,7,4,128]{3,2,1,0:T(4,128)(2,1)S(1)}, u32[]{:S(2)}, u32[]{:S(2)}) collective-permute-start(bf16[64,7,4,128]{3,2,1,0:T(4,128)(2,1)S(1)} %all_to_all.17.own_ref), channel_id=1, source_target_pairs={{0,8},{8,0},{1,9},{9,1},{2,10},{10,2},{3,11},{11,3},{4,12},{12,4},... | collective-permute-start | bytes 1376264 | tf_op jit(solution)/shard_map/ppermute | solution.py:215
  78.9 0.9 %copy.14 = bf16[2,14,14,384]{3,0,2,1:T(2,128)(2,1)} copy(bf16[2,14,14,384]{3,2,1,0:T(8,128)(2,1)S(1)} %input_grad.1) | data formatting | bytes 602112
  79.8 0.7 multiply_subtract_fusion
  80.5 0.0 collective-permute-done.1.got_ref
  80.5 1.3 %assemble.1 = bf16[384,1152]{1,0:T(8,128)(2,1)} custom-call(bf16[64,7,4,128]{3,2,1,0:T(4,128)(2,1)S(1)} %all_to_all.17.own_ref, bf16[64,7,4,128]{3,2,1,0:T(4,128)(2,1)S(1)} %collective-permute-done.1.got_ref), custom_call_target="tpu_custom_call" | custom-call | tf_op jit(solution)/shard_map/assemble/pallas_call | solution.py:283
  (5 shorter events, 0.1 us)
Async XLA Ops:
  0.6 1.1 %copy-start.5 = (bf16[2,14,14,384]{3,0,2,1:T(2,128)(2,1)S(1)}, bf16[2,14,14,384]{3,0,2,1:T(2,128)(2,1)}, u32[]{:S(2)}) copy-start(bf16[2,14,14,384]{3,0,2,1:T(2,128)(2,1)} %param.8) | copy-start | bytes 903172
  0.6 1.3 %copy-start = (bf16[384,1152]{1,0:T(8,128)(2,1)S(1)}, bf16[384,1152]{1,0:T(8,128)(2,1)}, u32[]{:S(2)}) copy-start(bf16[384,1152]{1,0:T(8,128)(2,1)} %k_ref.3) | copy-start | bytes 2654212
  4.1 10.2 %collective-permute-start = (bf16[64,7,4,128]{3,2,1,0:T(4,128)(2,1)S(1)}, bf16[64,7,4,128]{3,2,1,0:T(4,128)(2,1)S(1)}, u32[]{:S(2)}, u32[]{:S(2)}) collective-permute-start(bf16[64,7,4,128]{3,2,1,0:T(4,128)(2,1)S(1)} %get-tuple-element.13), channel_id=1, source_target_pairs={{0,8},{8,0},{1,9},{9,1},{2,10},{10,2},{3,11},{11,3},{4,12},{12,4},... | collective-permute-start | bytes 1376264 | tf_op jit(solution)/shard_map/ppermute | solution.py:215
  14.5 27.4 %copy-start.1 = (f32[864]{0:T(1024)S(1)}, f32[864]{0:T(1024)}, u32[]{:S(2)}) copy-start(f32[864]{0:T(1024)} %master_ref.1) | copy-start | bytes 10372
  14.5 27.4 %copy-start.2 = (f32[864]{0:T(1024)S(1)}, f32[864]{0:T(1024)}, u32[]{:S(2)}) copy-start(f32[864]{0:T(1024)} %mean_ref.1) | copy-start | bytes 10372
  14.5 27.3 %copy-start.3 = (f32[864]{0:T(1024)S(1)}, f32[864]{0:T(1024)}, u32[]{:S(2)}) copy-start(f32[864]{0:T(1024)} %square_ref.1) | copy-start | bytes 10372
  42.1 8.6 %copy-start.4 = (f32[384]{0:T(512)S(1)}, f32[384]{0:T(512)}, u32[]{:S(2)}) copy-start(f32[384]{0:T(512)} %gain_ref.1) | copy-start | bytes 4612
  71.8 8.7 %collective-permute-start.1 = (bf16[64,7,4,128]{3,2,1,0:T(4,128)(2,1)S(1)}, bf16[64,7,4,128]{3,2,1,0:T(4,128)(2,1)S(1)}, u32[]{:S(2)}, u32[]{:S(2)}) collective-permute-start(bf16[64,7,4,128]{3,2,1,0:T(4,128)(2,1)S(1)} %all_to_all.17.own_ref), channel_id=1, source_target_pairs={{0,8},{8,0},{1,9},{9,1},{2,10},{10,2},{3,11},{11,3},{4,12},{12,4},... | collective-permute-start | bytes 1376264 | tf_op jit(solution)/shard_map/ppermute | solution.py:215

commit v6 on v5

--- a/solution.py
+++ b/solution.py
@@ -27,7 +27,6 @@
 IMG = 256
 OUT = SIDE * 16
 VMEM = pl.BlockSpec(memory_space=pltpu.VMEM)
-SMEM = pl.BlockSpec(memory_space=pltpu.SMEM)
 
 
 def grant(mib):
@@ -131,12 +130,13 @@
     for i in range(1, 64):
         total = total + part_ref[i].astype(f32)
     for i in range(4):
-        out_ref[i, 24:56, :] = jnp.zeros((32, CG), f32)
         for k in range(TILES):
             out_ref[i, 4 * k : 4 * k + 4, :] = total[k]
+        for k in range(3):
+            out_ref[i, 33 + 7 * k : 34 + 7 * k, :] = jnp.zeros((1, CG), f32)
     for k, ref in enumerate((mean_ref, square_ref, master_ref)):
         for row in range(7):
-            at = 32 + 8 * k + row
+            at = USED + 7 * k + row
             some = min(CG, SHARD - row * CG)
             values = ref[pl.ds(row * CG, some)].reshape(1, some)
             for i in range(4):
@@ -153,30 +153,34 @@
 
 
 def adam_kernel(in_ref, gain_ref, grad_ref, send_ref, frame):
-    lane = lax.broadcasted_iota(jnp.int32, (8, CG), 1)
+    lane = lax.broadcasted_iota(jnp.int32, (7, CG), 1)
     frame[...] = jnp.zeros_like(frame)
     for p in range(4):
         base, shift = divmod(p * SHARD, CG)
         for k in range(3):
-            rows = in_ref[p, 32 + 8 * k : 40 + 8 * k, :]
+            rows = in_ref[p, USED + 7 * k : USED + 7 + 7 * k, :]
             if shift:
                 rows = pltpu.roll(rows, shift, 1)
-            frame[k, base : base + 8, :] += jnp.where(lane >= shift, rows, 0.0)
+            frame[k, base : base + 7, :] += jnp.where(lane >= shift, rows, 0.0)
             if shift:
-                frame[k, base + 1 : base + 9, :] += jnp.where(lane < shift, rows, 0.0)
-    grad = (in_ref[0, 0:32, :] + in_ref[1, 0:32, :]) + (in_ref[2, 0:32, :] + in_ref[3, 0:32, :])
-    grad_ref[...] = grad
-    master = adam(frame[0, 0:32, :], frame[1, 0:32, :], frame[2, 0:32, :], grad)[2]
-    row = lax.broadcasted_iota(jnp.int32, (32, CG), 0)
+                frame[k, base + 1 : base + 8, :] += jnp.where(lane < shift, rows, 0.0)
+    grad = (in_ref[0, 0:28, :] + in_ref[1, 0:28, :]) + (in_ref[2, 0:28, :] + in_ref[3, 0:28, :])
+    grad_ref[0:28, :] = grad
+    grad_ref[28:32, :] = jnp.zeros((4, CG), f32)
+    master = adam(frame[0, 0:28, :], frame[1, 0:28, :], frame[2, 0:28, :], grad)[2]
+    row = lax.broadcasted_iota(jnp.int32, (28, CG), 0)
+    index = lax.broadcasted_iota(jnp.int32, (3, CG), 0) * CG + lax.broadcasted_iota(jnp.int32, (3, CG), 1)
     block = (lax.axis_index("z") * 4 + lax.axis_index("yh")) * 4 + lax.axis_index("co") * 2 + lax.axis_index("yl")
-    mean_of = jnp.zeros((32, CG), f32)
-    scale_of = jnp.zeros((32, CG), f32)
+    mean_of = jnp.zeros((28, CG), f32)
+    scale_of = jnp.zeros((28, CG), f32)
     for r in range(3):
         mine = (row >= 9 * r) & (row < 9 * r + 9)
         values = jnp.where(mine, master, 0.0)
         mean = jnp.sum(jnp.sum(values, 0, keepdims=True), 1, keepdims=True) / FAN
         square = jnp.sum(jnp.sum(values * values, 0, keepdims=True), 1, keepdims=True) / FAN
-        scale = gain_ref[block * 3 + r] / jnp.sqrt(FAN * (square - mean * mean) + 0.0001)
+        picked = jnp.where(index == block * 3 + r, gain_ref[...], 0.0)
+        gain = jnp.sum(jnp.sum(picked, 0, keepdims=True), 1, keepdims=True)
+        scale = gain / jnp.sqrt(FAN * (square - mean * mean) + 0.0001)
         mean_of = jnp.where(mine, mean, mean_of)
         scale_of = jnp.where(mine, scale, scale_of)
     out = (master - mean_of) * scale_of
@@ -186,7 +190,7 @@
             send_ref[i, k] = tile
 
 
-def assemble_kernel(own_ref, got_ref, out_ref, blocks, taps):
+def assemble_kernel(own_ref, got_ref, out_ref, blocks, taps, rows, sems):
     me = lax.axis_index("co")
     for core in range(2):
 
@@ -200,11 +204,17 @@
                     blocks[kept + at : kept + at + some, :] = own_ref[q, k].astype(f32)[:some]
                     blocks[given + at : given + at + some, :] = got_ref[q, k].astype(f32)[:some]
 
-    for t in range(9):
-        for r in range(3):
-            taps[t, pl.ds(r, BLOCKS, 3), :] = blocks[pl.ds(9 * r + t, BLOCKS, USED), :]
-    for t in range(9):
-        out_ref[:, t * CG : (t + 1) * CG] = taps[t].astype(bf16)
+    copies = []
+    for part in range(3):
+        for t in range(3 * part, 3 * part + 3):
+            for r in range(3):
+                taps[t, pl.ds(r, BLOCKS, 3), :] = blocks[pl.ds(9 * r + t, BLOCKS, USED), :]
+            rows[part, :, (t - 3 * part) * CG : (t - 3 * part + 1) * CG] = taps[t].astype(bf16)
+        cols = pl.ds(part * 3 * CG, 3 * CG)
+        copies.append(pltpu.make_async_copy(rows.at[part], out_ref.at[:, cols], sems.at[part]))
+        copies[-1].start()
+    for copy in copies:
+        copy.wait()
 
 
 def shape(dims, dtype):
@@ -256,7 +266,7 @@
     parts = exchange(pair, ZY)
     payload = pl.pallas_call(
         reduce_kernel,
-        out_shape=shape((4, 56, CG), f32),
+        out_shape=shape((4, 48, CG), f32),
         in_specs=[VMEM] * 4,
         out_specs=VMEM,
         compiler_params=grant(4),
@@ -266,12 +276,12 @@
     grad, send = pl.pallas_call(
         adam_kernel,
         out_shape=(shape((ROWS, CG), f32), shape((64, TILES, 4, CG), bf16)),
-        in_specs=[VMEM, SMEM],
+        in_specs=[VMEM, VMEM],
         out_specs=(VMEM,) * 2,
         scratch_shapes=[pltpu.VMEM((3, 40, CG), f32)],
         compiler_params=grant(4),
         name="adam",
-    )(gathered, channel_gain)
+    )(gathered, channel_gain.reshape(3, CG))
     own = exchange(send, ZY)
     other = swap_cores(own)
     grad_shard = lax.dynamic_slice(
@@ -284,10 +294,12 @@
         assemble_kernel,
         out_shape=shape((CMID, FAN), bf16),
         in_specs=[VMEM] * 2,
-        out_specs=VMEM,
+        out_specs=pl.BlockSpec(memory_space=pl.ANY),
         scratch_shapes=[
             pltpu.VMEM((BLOCKS * USED + 8, CG), f32),
             pltpu.VMEM((9, CMID, CG), f32),
+            pltpu.VMEM((3, CMID, 3 * CG), bf16),
+            pltpu.SemaphoreType.DMA((3,)),
         ],
         compiler_params=grant(10),
         name="assemble",

time: 82.2 us -> 81.4 us (level)
  no operation moved by 1% of the time
where the time goes in v6:
time: 81.4 us; the launch traced here: 81 us
  blocking collectives  56.1 us (69%)
  starting transfers between devices  15.8 us (19%)
  Pallas kernels  4.78 us (6%)
  local copies, waits for them, and re-layouts  2.3 us (3%)
  other arithmetic  0.93 us (1%)
    all_to_all x3, blocking collectives, exchange(): return lax.all_to_all(x, axes, 0, 0, tiled=True)  56.1 us
    ppermute x2, starting transfers between devices, swap_cores(): return lax.ppermute(x, 'co', [(0, 1), (1, 0)])  15.8 us
    unnamed x15, local copies, waits for them, and re-layouts  2.3 us
    pallas_call x1, Pallas kernels, on_device(): pl.pallas_call(grads_kernel, out_shape=(shape((2 * IMG, CMID), bf16), sha...  2.11 us
  transfers between devices with their start and end apart: 2, of which 1 were waited for; matrix products, arithmetic and copies ran while one was open for 2% of the time, Pallas kernels for 1%

profile of v6, /device:TPU:1, one launch (start us, length us, event | category | flops | bytes accessed | tf_op | source)
XLA Modules:
  0.0 81.0 jit_solution(13674114576844807081)
XLA Ops:
  0.6 0.0 copy-start.5
  0.6 0.0 copy-start
  0.7 1.1 %copy.12.x_ref = bf16[2,14,14,384]{3,2,1,0:T(8,128)(2,1)S(1)} copy(bf16[2,14,14,384]{3,0,2,1:T(2,128)(2,1)} %param.7) | data formatting | bytes 602112 | tf_op args[0]
  1.8 0.0 copy-done.5
  1.8 0.2 copy-done
  2.0 2.1 %grads.1 = (bf16[512,384]{1,0:T(8,128)(2,1)S(1)}, bf16[64,7,4,128]{3,2,1,0:T(4,128)(2,1)S(1)}, bf16[64,7,4,128]{3,2,1,0:T(4,128)(2,1)S(1)}) custom-call(bf16[2,14,14,384]{3,2,1,0:T(8,128)(2,1)S(1)} %copy.12.x_ref, bf16[2,14,14,384]{3,2,1,0:T(8,128)(2,1)S(1)} %copy.13.cot_ref, bf16[384,1152]{1,0:T(8,128)(2,1)S(1)} %copy-done), custom_call_target="tpu_custom_call" | custom-call | tf_op jit(solution)/shard_map/grads/pallas_call | solution.py:235
  4.1 8.7 %collective-permute-start = (bf16[64,7,4,128]{3,2,1,0:T(4,128)(2,1)S(1)}, bf16[64,7,4,128]{3,2,1,0:T(4,128)(2,1)S(1)}, u32[]{:S(2)}, u32[]{:S(2)}) collective-permute-start(bf16[64,7,4,128]{3,2,1,0:T(4,128)(2,1)S(1)} %get-tuple-element.13), channel_id=1, source_target_pairs={{0,8},{8,0},{1,9},{9,1},{2,10},{10,2},{3,11},{11,3},{4,12},{12,4},... | collective-permute-start | bytes 1376264 | tf_op jit(solution)/shard_map/ppermute | solution.py:225
  12.9 1.0 %input_grad.1 = bf16[2,14,14,384]{3,2,1,0:T(8,128)(2,1)S(1)} custom-call(bf16[512,384]{1,0:T(8,128)(2,1)S(1)} %get-tuple-element.14.pg_ref, bf16[384,1152]{1,0:T(8,128)(2,1)S(1)} %copy-done), custom_call_target="tpu_custom_call" | custom-call | tf_op jit(solution)/shard_map/input_grad/pallas_call | solution.py:255
  13.9 0.4 collective-permute-done
  14.3 0.2 add_convert_fusion
  14.5 0.0 copy-start.1
  14.5 0.0 copy-start.2
  14.5 0.0 copy-start.3
  14.6 27.3 %all_to_all.15.part_ref = bf16[64,7,4,128]{3,2,1,0:T(4,128)(2,1)S(1)} all-to-all(bf16[64,7,4,128]{3,2,1,0:T(4,128)(2,1)S(1)} %add_convert_fusion), channel_id=1, replica_groups=mesh['z'=8,'yh'=4,'co'=2,'yl'=2,'x'=4] {'z','yh','yl'}, dimensions={0} | all-to-all | bytes 917504 | tf_op jit(solution)/shard_map/all_to_all | solution.py:229
  41.9 0.0 copy-done.1
  41.9 0.2 reduce.1
  42.1 8.5 %all_to_all.16.in_ref = f32[4,48,128]{2,1,0:T(8,128)S(1)} all-to-all(f32[4,48,128]{2,1,0:T(8,128)S(1)} %reduce.1), channel_id=1, replica_groups=mesh['z'=8,'yh'=4,'co'=2,'yl'=2,'x'=4] {'x'}, dimensions={0} | all-to-all | bytes 196608 | tf_op jit(solution)/shard_map/all_to_all | solution.py:229
  50.5 0.3 adam.1
  50.9 20.3 %all_to_all.17.own_ref = bf16[64,7,4,128]{3,2,1,0:T(4,128)(2,1)S(1)} all-to-all(bf16[64,7,4,128]{3,2,1,0:T(4,128)(2,1)S(1)} %get-tuple-element.18), channel_id=1, replica_groups=mesh['z'=8,'yh'=4,'co'=2,'yl'=2,'x'=4] {'z','yh','yl'}, dimensions={0} | all-to-all | bytes 917504 | tf_op jit(solution)/shard_map/all_to_all | solution.py:229
  71.2 7.0 %collective-permute-start.1 = (bf16[64,7,4,128]{3,2,1,0:T(4,128)(2,1)S(1)}, bf16[64,7,4,128]{3,2,1,0:T(4,128)(2,1)S(1)}, u32[]{:S(2)}, u32[]{:S(2)}) collective-permute-start(bf16[64,7,4,128]{3,2,1,0:T(4,128)(2,1)S(1)} %all_to_all.17.own_ref), channel_id=1, source_target_pairs={{0,8},{8,0},{1,9},{9,1},{2,10},{10,2},{3,11},{11,3},{4,12},{12,4},... | collective-permute-start | bytes 1376264 | tf_op jit(solution)/shard_map/ppermute | solution.py:225
  78.2 0.9 %copy.14 = bf16[2,14,14,384]{3,0,2,1:T(2,128)(2,1)} copy(bf16[2,14,14,384]{3,2,1,0:T(8,128)(2,1)S(1)} %input_grad.1) | data formatting | bytes 602112
  79.2 0.7 multiply_subtract_fusion
  79.9 0.0 collective-permute-done.1.got_ref
  79.9 1.2 %assemble.1 = bf16[384,1152]{1,0:T(8,128)(2,1)} custom-call(bf16[64,7,4,128]{3,2,1,0:T(4,128)(2,1)S(1)} %all_to_all.17.own_ref, bf16[64,7,4,128]{3,2,1,0:T(4,128)(2,1)S(1)} %collective-permute-done.1.got_ref), custom_call_target="tpu_custom_call" | custom-call | tf_op jit(solution)/shard_map/assemble/pallas_call | solution.py:293
  (5 shorter events, 0.1 us)
Async XLA Ops:
  0.6 1.1 %copy-start.5 = (bf16[2,14,14,384]{3,0,2,1:T(2,128)(2,1)S(1)}, bf16[2,14,14,384]{3,0,2,1:T(2,128)(2,1)}, u32[]{:S(2)}) copy-start(bf16[2,14,14,384]{3,0,2,1:T(2,128)(2,1)} %param.8) | copy-start | bytes 903172
  0.6 1.3 %copy-start = (bf16[384,1152]{1,0:T(8,128)(2,1)S(1)}, bf16[384,1152]{1,0:T(8,128)(2,1)}, u32[]{:S(2)}) copy-start(bf16[384,1152]{1,0:T(8,128)(2,1)} %k_ref.3) | copy-start | bytes 2654212
  4.1 10.2 %collective-permute-start = (bf16[64,7,4,128]{3,2,1,0:T(4,128)(2,1)S(1)}, bf16[64,7,4,128]{3,2,1,0:T(4,128)(2,1)S(1)}, u32[]{:S(2)}, u32[]{:S(2)}) collective-permute-start(bf16[64,7,4,128]{3,2,1,0:T(4,128)(2,1)S(1)} %get-tuple-element.13), channel_id=1, source_target_pairs={{0,8},{8,0},{1,9},{9,1},{2,10},{10,2},{3,11},{11,3},{4,12},{12,4},... | collective-permute-start | bytes 1376264 | tf_op jit(solution)/shard_map/ppermute | solution.py:225
  14.5 27.4 %copy-start.1 = (f32[864]{0:T(1024)S(1)}, f32[864]{0:T(1024)}, u32[]{:S(2)}) copy-start(f32[864]{0:T(1024)} %master_ref.1) | copy-start | bytes 10372
  14.5 27.4 %copy-start.2 = (f32[864]{0:T(1024)S(1)}, f32[864]{0:T(1024)}, u32[]{:S(2)}) copy-start(f32[864]{0:T(1024)} %mean_ref.1) | copy-start | bytes 10372
  14.5 27.3 %copy-start.3 = (f32[864]{0:T(1024)S(1)}, f32[864]{0:T(1024)}, u32[]{:S(2)}) copy-start(f32[864]{0:T(1024)} %square_ref.1) | copy-start | bytes 10372
  42.1 8.5 %copy-start.4 = (f32[384]{0:T(512)S(1)}, f32[384]{0:T(512)}, u32[]{:S(2)}) copy-start(f32[384]{0:T(512)} %param.10) | copy-start | bytes 4612
  71.2 8.7 %collective-permute-start.1 = (bf16[64,7,4,128]{3,2,1,0:T(4,128)(2,1)S(1)}, bf16[64,7,4,128]{3,2,1,0:T(4,128)(2,1)S(1)}, u32[]{:S(2)}, u32[]{:S(2)}) collective-permute-start(bf16[64,7,4,128]{3,2,1,0:T(4,128)(2,1)S(1)} %all_to_all.17.own_ref), channel_id=1, source_target_pairs={{0,8},{8,0},{1,9},{9,1},{2,10},{10,2},{3,11},{11,3},{4,12},{12,4},... | collective-permute-start | bytes 1376264 | tf_op jit(solution)/shard_map/ppermute | solution.py:225

commit v7 on v6

--- a/solution.py
+++ b/solution.py
@@ -57,7 +57,7 @@
     return jnp.concatenate([cells.astype(f32), jnp.zeros((2, CMID), f32)], 0)
 
 
-def grads_kernel(x_ref, cot_ref, k_ref, pg_ref, keep_ref, give_ref, xf, xs, cf, taps, blocks):
+def grads_kernel(x_ref, cot_ref, k_ref, pg_ref, blocks, give_ref, xf, xs, cf, taps):
     me = lax.axis_index("co")
     for n in range(2):
         for at in (n * IMG, n * IMG + 240):
@@ -104,15 +104,24 @@
         @pl.when(me == core)
         def _():
             for q in range(64):
-                kept = (q // 2 * 4 + 2 * core + q % 2) * USED
                 given = (q // 2 * 4 + 2 - 2 * core + q % 2) * USED
                 for k in range(TILES):
-                    at = 4 * k
-                    keep_ref[q, k] = blocks[kept + at : kept + at + 4, :].astype(bf16)
-                    give_ref[q, k] = blocks[given + at : given + at + 4, :].astype(bf16)
-
-
-def input_kernel(pg_ref, k_ref, out_ref, ps):
+                    at = given + 4 * k
+                    give_ref[q, k] = blocks[at : at + 4, :].astype(bf16)
+
+
+def input_kernel(pg_ref, k_ref, blocks, out_ref, keep_ref, ps):
+    me = lax.axis_index("co")
+    for core in range(2):
+
+        @pl.when(me == core)
+        def _():
+            for q in range(64):
+                kept = (q // 2 * 4 + 2 * core + q % 2) * USED
+                for k in range(TILES):
+                    at = kept + 4 * k
+                    keep_ref[q, k] = blocks[at : at + 4, :].astype(bf16)
+
     shift_columns(pg_ref[...].astype(f32), ps)
     for g in range(GROUPS):
         cols = slice(g * CG, (g + 1) * CG)
@@ -205,13 +214,12 @@
                     blocks[given + at : given + at + some, :] = got_ref[q, k].astype(f32)[:some]
 
     copies = []
-    for part in range(3):
-        for t in range(3 * part, 3 * part + 3):
-            for r in range(3):
-                taps[t, pl.ds(r, BLOCKS, 3), :] = blocks[pl.ds(9 * r + t, BLOCKS, USED), :]
-            rows[part, :, (t - 3 * part) * CG : (t - 3 * part + 1) * CG] = taps[t].astype(bf16)
-        cols = pl.ds(part * 3 * CG, 3 * CG)
-        copies.append(pltpu.make_async_copy(rows.at[part], out_ref.at[:, cols], sems.at[part]))
+    for t in range(9):
+        for r in range(3):
+            taps[t, pl.ds(r, BLOCKS, 3), :] = blocks[pl.ds(9 * r + t, BLOCKS, USED), :]
+        rows[t] = taps[t].astype(bf16)
+        cols = pl.ds(t * CG, CG)
+        copies.append(pltpu.make_async_copy(rows.at[t], out_ref.at[:, cols], sems.at[t]))
         copies[-1].start()
     for copy in copies:
         copy.wait()
@@ -232,11 +240,11 @@
 def on_device(
     activations, cotangent, kernel, channel_gain, master_flat, moment_mean, moment_square
 ):
-    pre_grad, keep, give = pl.pallas_call(
+    pre_grad, blocks, give = pl.pallas_call(
         grads_kernel,
         out_shape=(
             shape((2 * IMG, CMID), bf16),
-            shape((64, TILES, 4, CG), bf16),
+            shape((BLOCKS * USED + 8, CG), f32),
             shape((64, TILES, 4, CG), bf16),
         ),
         in_specs=[VMEM] * 3,
@@ -246,23 +254,21 @@
             pltpu.VMEM((3, 2 * IMG, CMID), bf16),
             pltpu.VMEM((2 * OUT, CMID), f32),
             pltpu.VMEM((9, CMID, CG), f32),
-            pltpu.VMEM((BLOCKS * USED + 8, CG), f32),
         ],
         compiler_params=grant(20),
         name="grads",
     )(activations, cotangent, kernel)
     got = swap_cores(give)
-    input_grad = pl.pallas_call(
+    input_grad, keep = pl.pallas_call(
         input_kernel,
-        out_shape=shape((2, SIDE, SIDE, CMID), bf16),
-        in_specs=[VMEM] * 2,
-        out_specs=VMEM,
+        out_shape=(shape((2, SIDE, SIDE, CMID), bf16), shape((64, TILES, 4, CG), bf16)),
+        in_specs=[VMEM] * 3,
+        out_specs=(VMEM,) * 2,
         scratch_shapes=[pltpu.VMEM((3, 2 * IMG, CMID), bf16)],
         compiler_params=grant(12),
         name="input_grad",
-    )(pre_grad, kernel)
+    )(pre_grad, kernel, blocks)
     pair = (keep.astype(f32) + got.astype(f32)).astype(bf16)
-    pair, input_grad = lax.optimization_barrier((pair, input_grad))
     parts = exchange(pair, ZY)
     payload = pl.pallas_call(
         reduce_kernel,
@@ -298,8 +304,8 @@
         scratch_shapes=[
             pltpu.VMEM((BLOCKS * USED + 8, CG), f32),
             pltpu.VMEM((9, CMID, CG), f32),
-            pltpu.VMEM((3, CMID, 3 * CG), bf16),
-            pltpu.SemaphoreType.DMA((3,)),
+            pltpu.VMEM((9, CMID, CG), bf16),
+            pltpu.SemaphoreType.DMA((9,)),
         ],
         compiler_params=grant(10),
         name="assemble",

time: 81.4 us -> 81.7 us (level)
    unnamed x15 -> x13, local copies, waits for them, and re-layouts: 2.3 us -> 3.08 us
where the time goes in v7:
time: 81.7 us; the launch traced here: 81.5 us
  blocking collectives  56 us (69%)
  starting transfers between devices  15.8 us (19%)
  Pallas kernels  4.78 us (6%)
  local copies, waits for them, and re-layouts  3.08 us (4%)
  other arithmetic  0.93 us (1%)
    all_to_all x3, blocking collectives, exchange(): return lax.all_to_all(x, axes, 0, 0, tiled=True)  56 us
    ppermute x2, starting transfers between devices, swap_cores(): return lax.ppermute(x, 'co', [(0, 1), (1, 0)])  15.8 us
    unnamed x13, local copies, waits for them, and re-layouts  3.08 us
    pallas_call x1, Pallas kernels, on_device(): pl.pallas_call(grads_kernel, out_shape=(shape((2 * IMG, CMID), bf16), sha...  1.95 us
  transfers between devices with their start and end apart: 2, of which 1 were waited for; matrix products, arithmetic and copies ran while one was open for 2% of the time, Pallas kernels for 1%

profile of v7, /device:TPU:1, one launch (start us, length us, event | category | flops | bytes accessed | tf_op | source)
XLA Modules:
  0.0 81.5 jit_solution(10803603688200672263)
XLA Ops:
  0.6 0.0 copy-start
  0.6 1.1 %copy.12.x_ref = bf16[2,14,14,384]{3,2,1,0:T(8,128)(2,1)S(1)} copy(bf16[2,14,14,384]{3,0,2,1:T(2,128)(2,1)} %param.7) | data formatting | bytes 602112 | tf_op args[0]
  1.7 1.0 %copy.13.cot_ref = bf16[2,14,14,384]{3,2,1,0:T(8,128)(2,1)S(1)} copy(bf16[2,14,14,384]{3,0,2,1:T(2,128)(2,1)} %param.8) | data formatting | bytes 602112 | tf_op args[1]
  2.8 0.0 copy-done
  2.8 2.0 %grads.1 = (bf16[512,384]{1,0:T(8,128)(2,1)S(1)}, f32[3464,128]{1,0:T(8,128)S(1)}, bf16[64,7,4,128]{3,2,1,0:T(4,128)(2,1)S(1)}) custom-call(bf16[2,14,14,384]{3,2,1,0:T(8,128)(2,1)S(1)} %copy.12.x_ref, bf16[2,14,14,384]{3,2,1,0:T(8,128)(2,1)S(1)} %copy.13.cot_ref, bf16[384,1152]{1,0:T(8,128)(2,1)S(1)} %copy-done), custom_call_target="tpu_custom_call" | custom-call | tf_op jit(solution)/shard_map/grads/pallas_call | solution.py:243
  4.7 8.7 %collective-permute-start = (bf16[64,7,4,128]{3,2,1,0:T(4,128)(2,1)S(1)}, bf16[64,7,4,128]{3,2,1,0:T(4,128)(2,1)S(1)}, u32[]{:S(2)}, u32[]{:S(2)}) collective-permute-start(bf16[64,7,4,128]{3,2,1,0:T(4,128)(2,1)S(1)} %get-tuple-element.16), channel_id=1, source_target_pairs={{0,8},{8,0},{1,9},{9,1},{2,10},{10,2},{3,11},{11,3},{4,12},{12,4},... | collective-permute-start | bytes 1376264 | tf_op jit(solution)/shard_map/ppermute | solution.py:233
  13.5 1.2 %input_grad.1 = (bf16[2,14,14,384]{3,2,1,0:T(8,128)(2,1)S(1)}, bf16[64,7,4,128]{3,2,1,0:T(4,128)(2,1)S(1)}) custom-call(bf16[512,384]{1,0:T(8,128)(2,1)S(1)} %get-tuple-element.12.pg_ref, bf16[384,1152]{1,0:T(8,128)(2,1)S(1)} %copy-done, f32[3464,128]{1,0:T(8,128)S(1)} %get-tuple-element.13.blocks), custom_call_target="tpu_custom_call" | custom-call | tf_op jit(solution)/shard_map/input_grad/pallas_call | solution.py:262
  14.6 0.0 copy-start.1
  14.7 0.0 copy-start.2
  14.7 0.0 copy-start.3
  14.7 0.0 copy-start.4
  14.7 0.2 collective-permute-done
  14.9 0.2 add_convert_fusion
  15.1 27.2 %all_to_all.15.part_ref = bf16[64,7,4,128]{3,2,1,0:T(4,128)(2,1)S(1)} all-to-all(bf16[64,7,4,128]{3,2,1,0:T(4,128)(2,1)S(1)} %add_convert_fusion), channel_id=1, replica_groups=mesh['z'=8,'yh'=4,'co'=2,'yl'=2,'x'=4] {'z','yh','yl'}, dimensions={0} | all-to-all | bytes 917504 | tf_op jit(solution)/shard_map/all_to_all | solution.py:237
  42.3 0.0 copy-done.2
  42.3 0.2 reduce.1
  42.5 8.5 %all_to_all.16.in_ref = f32[4,48,128]{2,1,0:T(8,128)S(1)} all-to-all(f32[4,48,128]{2,1,0:T(8,128)S(1)} %reduce.1), channel_id=1, replica_groups=mesh['z'=8,'yh'=4,'co'=2,'yl'=2,'x'=4] {'x'}, dimensions={0} | all-to-all | bytes 196608 | tf_op jit(solution)/shard_map/all_to_all | solution.py:237
  51.0 0.3 adam.1
  51.3 20.3 %all_to_all.17.own_ref = bf16[64,7,4,128]{3,2,1,0:T(4,128)(2,1)S(1)} all-to-all(bf16[64,7,4,128]{3,2,1,0:T(4,128)(2,1)S(1)} %get-tuple-element.18), channel_id=1, replica_groups=mesh['z'=8,'yh'=4,'co'=2,'yl'=2,'x'=4] {'z','yh','yl'}, dimensions={0} | all-to-all | bytes 917504 | tf_op jit(solution)/shard_map/all_to_all | solution.py:237
  71.6 7.0 %collective-permute-start.1 = (bf16[64,7,4,128]{3,2,1,0:T(4,128)(2,1)S(1)}, bf16[64,7,4,128]{3,2,1,0:T(4,128)(2,1)S(1)}, u32[]{:S(2)}, u32[]{:S(2)}) collective-permute-start(bf16[64,7,4,128]{3,2,1,0:T(4,128)(2,1)S(1)} %all_to_all.17.own_ref), channel_id=1, source_target_pairs={{0,8},{8,0},{1,9},{9,1},{2,10},{10,2},{3,11},{11,3},{4,12},{12,4},... | collective-permute-start | bytes 1376264 | tf_op jit(solution)/shard_map/ppermute | solution.py:233
  78.7 0.9 %copy.14 = bf16[2,14,14,384]{3,0,2,1:T(2,128)(2,1)} copy(bf16[2,14,14,384]{3,2,1,0:T(8,128)(2,1)S(1)} %get-tuple-element.19) | data formatting | bytes 602112
  79.6 0.7 multiply_subtract_fusion
  80.3 0.0 collective-permute-done.1.got_ref
  80.3 1.1 %assemble.1 = bf16[384,1152]{1,0:T(8,128)(2,1)} custom-call(bf16[64,7,4,128]{3,2,1,0:T(4,128)(2,1)S(1)} %all_to_all.17.own_ref, bf16[64,7,4,128]{3,2,1,0:T(4,128)(2,1)S(1)} %collective-permute-done.1.got_ref), custom_call_target="tpu_custom_call" | custom-call | tf_op jit(solution)/shard_map/assemble/pallas_call | solution.py:299
  (3 shorter events, 0.0 us)
Async XLA Ops:
  0.6 2.1 %copy-start = (bf16[384,1152]{1,0:T(8,128)(2,1)S(1)}, bf16[384,1152]{1,0:T(8,128)(2,1)}, u32[]{:S(2)}) copy-start(bf16[384,1152]{1,0:T(8,128)(2,1)} %k_ref.3) | copy-start | bytes 2654212
  4.7 10.2 %collective-permute-start = (bf16[64,7,4,128]{3,2,1,0:T(4,128)(2,1)S(1)}, bf16[64,7,4,128]{3,2,1,0:T(4,128)(2,1)S(1)}, u32[]{:S(2)}, u32[]{:S(2)}) collective-permute-start(bf16[64,7,4,128]{3,2,1,0:T(4,128)(2,1)S(1)} %get-tuple-element.16), channel_id=1, source_target_pairs={{0,8},{8,0},{1,9},{9,1},{2,10},{10,2},{3,11},{11,3},{4,12},{12,4},... | collective-permute-start | bytes 1376264 | tf_op jit(solution)/shard_map/ppermute | solution.py:233
  14.6 27.7 %copy-start.1 = (f32[864]{0:T(1024)S(1)}, f32[864]{0:T(1024)}, u32[]{:S(2)}) copy-start(f32[864]{0:T(1024)} %master_ref.1) | copy-start | bytes 10372
  14.7 27.7 %copy-start.2 = (f32[864]{0:T(1024)S(1)}, f32[864]{0:T(1024)}, u32[]{:S(2)}) copy-start(f32[864]{0:T(1024)} %mean_ref.1) | copy-start | bytes 10372
  14.7 27.7 %copy-start.3 = (f32[864]{0:T(1024)S(1)}, f32[864]{0:T(1024)}, u32[]{:S(2)}) copy-start(f32[864]{0:T(1024)} %square_ref.1) | copy-start | bytes 10372
  14.7 36.3 %copy-start.4 = (f32[384]{0:T(512)S(1)}, f32[384]{0:T(512)}, u32[]{:S(2)}) copy-start(f32[384]{0:T(512)} %param.10) | copy-start | bytes 4612
  71.6 8.7 %collective-permute-start.1 = (bf16[64,7,4,128]{3,2,1,0:T(4,128)(2,1)S(1)}, bf16[64,7,4,128]{3,2,1,0:T(4,128)(2,1)S(1)}, u32[]{:S(2)}, u32[]{:S(2)}) collective-permute-start(bf16[64,7,4,128]{3,2,1,0:T(4,128)(2,1)S(1)} %all_to_all.17.own_ref), channel_id=1, source_target_pairs={{0,8},{8,0},{1,9},{9,1},{2,10},{10,2},{3,11},{11,3},{4,12},{12,4},... | collective-permute-start | bytes 1376264 | tf_op jit(solution)/shard_map/ppermute | solution.py:233

commit v8 on v6

--- a/solution.py
+++ b/solution.py
@@ -205,13 +205,12 @@
                     blocks[given + at : given + at + some, :] = got_ref[q, k].astype(f32)[:some]
 
     copies = []
-    for part in range(3):
-        for t in range(3 * part, 3 * part + 3):
-            for r in range(3):
-                taps[t, pl.ds(r, BLOCKS, 3), :] = blocks[pl.ds(9 * r + t, BLOCKS, USED), :]
-            rows[part, :, (t - 3 * part) * CG : (t - 3 * part + 1) * CG] = taps[t].astype(bf16)
-        cols = pl.ds(part * 3 * CG, 3 * CG)
-        copies.append(pltpu.make_async_copy(rows.at[part], out_ref.at[:, cols], sems.at[part]))
+    for t in range(9):
+        for r in range(3):
+            taps[t, pl.ds(r, BLOCKS, 3), :] = blocks[pl.ds(9 * r + t, BLOCKS, USED), :]
+        rows[t] = taps[t].astype(bf16)
+        cols = pl.ds(t * CG, CG)
+        copies.append(pltpu.make_async_copy(rows.at[t], out_ref.at[:, cols], sems.at[t]))
         copies[-1].start()
     for copy in copies:
         copy.wait()
@@ -298,8 +297,8 @@
         scratch_shapes=[
             pltpu.VMEM((BLOCKS * USED + 8, CG), f32),
             pltpu.VMEM((9, CMID, CG), f32),
-            pltpu.VMEM((3, CMID, 3 * CG), bf16),
-            pltpu.SemaphoreType.DMA((3,)),
+            pltpu.VMEM((9, CMID, CG), bf16),
+            pltpu.SemaphoreType.DMA((9,)),
         ],
         compiler_params=grant(10),
         name="assemble",

time: 81.4 us -> 81.3 us (level)
  no operation moved by 1% of the time
where the time goes in v8:
time: 81.3 us; the launch traced here: 81 us
  blocking collectives  56.1 us (69%)
  starting transfers between devices  15.8 us (19%)
  Pallas kernels  4.76 us (6%)
  local copies, waits for them, and re-layouts  2.3 us (3%)
  other arithmetic  0.93 us (1%)
    all_to_all x3, blocking collectives, exchange(): return lax.all_to_all(x, axes, 0, 0, tiled=True)  56.1 us
    ppermute x2, starting transfers between devices, swap_cores(): return lax.ppermute(x, 'co', [(0, 1), (1, 0)])  15.8 us
    unnamed x15, local copies, waits for them, and re-layouts  2.3 us
    pallas_call x1, Pallas kernels, on_device(): pl.pallas_call(grads_kernel, out_shape=(shape((2 * IMG, CMID), bf16), sha...  2.11 us
  transfers between devices with their start and end apart: 2, of which 1 were waited for; matrix products, arithmetic and copies ran while one was open for 2% of the time, Pallas kernels for 1%

profile of v8, /device:TPU:1, one launch (start us, length us, event | category | flops | bytes accessed | tf_op | source)
XLA Modules:
  0.0 81.0 jit_solution(8862844066686883331)
XLA Ops:
  0.6 0.0 copy-start.5
  0.6 0.0 copy-start
  0.7 1.1 %copy.12.x_ref = bf16[2,14,14,384]{3,2,1,0:T(8,128)(2,1)S(1)} copy(bf16[2,14,14,384]{3,0,2,1:T(2,128)(2,1)} %param.7) | data formatting | bytes 602112 | tf_op args[0]
  1.8 0.0 copy-done.5
  1.8 0.2 copy-done
  2.0 2.1 %grads.1 = (bf16[512,384]{1,0:T(8,128)(2,1)S(1)}, bf16[64,7,4,128]{3,2,1,0:T(4,128)(2,1)S(1)}, bf16[64,7,4,128]{3,2,1,0:T(4,128)(2,1)S(1)}) custom-call(bf16[2,14,14,384]{3,2,1,0:T(8,128)(2,1)S(1)} %copy.12.x_ref, bf16[2,14,14,384]{3,2,1,0:T(8,128)(2,1)S(1)} %copy.13.cot_ref, bf16[384,1152]{1,0:T(8,128)(2,1)S(1)} %copy-done), custom_call_target="tpu_custom_call" | custom-call | tf_op jit(solution)/shard_map/grads/pallas_call | solution.py:234
  4.1 8.7 %collective-permute-start = (bf16[64,7,4,128]{3,2,1,0:T(4,128)(2,1)S(1)}, bf16[64,7,4,128]{3,2,1,0:T(4,128)(2,1)S(1)}, u32[]{:S(2)}, u32[]{:S(2)}) collective-permute-start(bf16[64,7,4,128]{3,2,1,0:T(4,128)(2,1)S(1)} %get-tuple-element.13), channel_id=1, source_target_pairs={{0,8},{8,0},{1,9},{9,1},{2,10},{10,2},{3,11},{11,3},{4,12},{12,4},... | collective-permute-start | bytes 1376264 | tf_op jit(solution)/shard_map/ppermute | solution.py:224
  12.9 1.0 %input_grad.1 = bf16[2,14,14,384]{3,2,1,0:T(8,128)(2,1)S(1)} custom-call(bf16[512,384]{1,0:T(8,128)(2,1)S(1)} %get-tuple-element.14.pg_ref, bf16[384,1152]{1,0:T(8,128)(2,1)S(1)} %copy-done), custom_call_target="tpu_custom_call" | custom-call | tf_op jit(solution)/shard_map/input_grad/pallas_call | solution.py:254
  13.9 0.4 collective-permute-done
  14.3 0.2 add_convert_fusion
  14.5 0.0 copy-start.1
  14.5 0.0 copy-start.2
  14.5 0.0 copy-start.3
  14.6 27.3 %all_to_all.15.part_ref = bf16[64,7,4,128]{3,2,1,0:T(4,128)(2,1)S(1)} all-to-all(bf16[64,7,4,128]{3,2,1,0:T(4,128)(2,1)S(1)} %add_convert_fusion), channel_id=1, replica_groups=mesh['z'=8,'yh'=4,'co'=2,'yl'=2,'x'=4] {'z','yh','yl'}, dimensions={0} | all-to-all | bytes 917504 | tf_op jit(solution)/shard_map/all_to_all | solution.py:228
  41.9 0.0 copy-done.1
  41.9 0.2 reduce.1
  42.1 8.5 %all_to_all.16.in_ref = f32[4,48,128]{2,1,0:T(8,128)S(1)} all-to-all(f32[4,48,128]{2,1,0:T(8,128)S(1)} %reduce.1), channel_id=1, replica_groups=mesh['z'=8,'yh'=4,'co'=2,'yl'=2,'x'=4] {'x'}, dimensions={0} | all-to-all | bytes 196608 | tf_op jit(solution)/shard_map/all_to_all | solution.py:228
  50.5 0.3 adam.1
  50.9 20.3 %all_to_all.17.own_ref = bf16[64,7,4,128]{3,2,1,0:T(4,128)(2,1)S(1)} all-to-all(bf16[64,7,4,128]{3,2,1,0:T(4,128)(2,1)S(1)} %get-tuple-element.18), channel_id=1, replica_groups=mesh['z'=8,'yh'=4,'co'=2,'yl'=2,'x'=4] {'z','yh','yl'}, dimensions={0} | all-to-all | bytes 917504 | tf_op jit(solution)/shard_map/all_to_all | solution.py:228
  71.2 7.0 %collective-permute-start.1 = (bf16[64,7,4,128]{3,2,1,0:T(4,128)(2,1)S(1)}, bf16[64,7,4,128]{3,2,1,0:T(4,128)(2,1)S(1)}, u32[]{:S(2)}, u32[]{:S(2)}) collective-permute-start(bf16[64,7,4,128]{3,2,1,0:T(4,128)(2,1)S(1)} %all_to_all.17.own_ref), channel_id=1, source_target_pairs={{0,8},{8,0},{1,9},{9,1},{2,10},{10,2},{3,11},{11,3},{4,12},{12,4},... | collective-permute-start | bytes 1376264 | tf_op jit(solution)/shard_map/ppermute | solution.py:224
  78.2 0.9 %copy.14 = bf16[2,14,14,384]{3,0,2,1:T(2,128)(2,1)} copy(bf16[2,14,14,384]{3,2,1,0:T(8,128)(2,1)S(1)} %input_grad.1) | data formatting | bytes 602112
  79.2 0.7 multiply_subtract_fusion
  79.9 0.0 collective-permute-done.1.got_ref
  79.9 1.1 %assemble.1 = bf16[384,1152]{1,0:T(8,128)(2,1)} custom-call(bf16[64,7,4,128]{3,2,1,0:T(4,128)(2,1)S(1)} %all_to_all.17.own_ref, bf16[64,7,4,128]{3,2,1,0:T(4,128)(2,1)S(1)} %collective-permute-done.1.got_ref), custom_call_target="tpu_custom_call" | custom-call | tf_op jit(solution)/shard_map/assemble/pallas_call | solution.py:292
  (5 shorter events, 0.1 us)
Async XLA Ops:
  0.6 1.1 %copy-start.5 = (bf16[2,14,14,384]{3,0,2,1:T(2,128)(2,1)S(1)}, bf16[2,14,14,384]{3,0,2,1:T(2,128)(2,1)}, u32[]{:S(2)}) copy-start(bf16[2,14,14,384]{3,0,2,1:T(2,128)(2,1)} %param.8) | copy-start | bytes 903172
  0.6 1.3 %copy-start = (bf16[384,1152]{1,0:T(8,128)(2,1)S(1)}, bf16[384,1152]{1,0:T(8,128)(2,1)}, u32[]{:S(2)}) copy-start(bf16[384,1152]{1,0:T(8,128)(2,1)} %k_ref.3) | copy-start | bytes 2654212
  4.1 10.2 %collective-permute-start = (bf16[64,7,4,128]{3,2,1,0:T(4,128)(2,1)S(1)}, bf16[64,7,4,128]{3,2,1,0:T(4,128)(2,1)S(1)}, u32[]{:S(2)}, u32[]{:S(2)}) collective-permute-start(bf16[64,7,4,128]{3,2,1,0:T(4,128)(2,1)S(1)} %get-tuple-element.13), channel_id=1, source_target_pairs={{0,8},{8,0},{1,9},{9,1},{2,10},{10,2},{3,11},{11,3},{4,12},{12,4},... | collective-permute-start | bytes 1376264 | tf_op jit(solution)/shard_map/ppermute | solution.py:224
  14.5 27.4 %copy-start.1 = (f32[864]{0:T(1024)S(1)}, f32[864]{0:T(1024)}, u32[]{:S(2)}) copy-start(f32[864]{0:T(1024)} %master_ref.1) | copy-start | bytes 10372
  14.5 27.4 %copy-start.2 = (f32[864]{0:T(1024)S(1)}, f32[864]{0:T(1024)}, u32[]{:S(2)}) copy-start(f32[864]{0:T(1024)} %mean_ref.1) | copy-start | bytes 10372
  14.5 27.3 %copy-start.3 = (f32[864]{0:T(1024)S(1)}, f32[864]{0:T(1024)}, u32[]{:S(2)}) copy-start(f32[864]{0:T(1024)} %square_ref.1) | copy-start | bytes 10372
  42.1 8.5 %copy-start.4 = (f32[384]{0:T(512)S(1)}, f32[384]{0:T(512)}, u32[]{:S(2)}) copy-start(f32[384]{0:T(512)} %param.10) | copy-start | bytes 4612
  71.2 8.7 %collective-permute-start.1 = (bf16[64,7,4,128]{3,2,1,0:T(4,128)(2,1)S(1)}, bf16[64,7,4,128]{3,2,1,0:T(4,128)(2,1)S(1)}, u32[]{:S(2)}, u32[]{:S(2)}) collective-permute-start(bf16[64,7,4,128]{3,2,1,0:T(4,128)(2,1)S(1)} %all_to_all.17.own_ref), channel_id=1, source_target_pairs={{0,8},{8,0},{1,9},{9,1},{2,10},{10,2},{3,11},{11,3},{4,12},{12,4},... | collective-permute-start | bytes 1376264 | tf_op jit(solution)/shard_map/ppermute | solution.py:224

commit v9 on v6

--- a/solution.py
+++ b/solution.py
@@ -126,9 +126,10 @@
 
 
 def reduce_kernel(part_ref, mean_ref, square_ref, master_ref, out_ref):
-    total = part_ref[0].astype(f32)
-    for i in range(1, 64):
-        total = total + part_ref[i].astype(f32)
+    sums = [part_ref[i].astype(f32) for i in range(4)]
+    for i in range(4, 64):
+        sums[i % 4] = sums[i % 4] + part_ref[i].astype(f32)
+    total = (sums[0] + sums[1]) + (sums[2] + sums[3])
     for i in range(4):
         for k in range(TILES):
             out_ref[i, 4 * k : 4 * k + 4, :] = total[k]

time: 81.4 us -> 81.3 us (level)
  no operation moved by 1% of the time
where the time goes in v9:
time: 81.3 us; the launch traced here: 81 us
  blocking collectives  56.1 us (69%)
  starting transfers between devices  15.8 us (19%)
  Pallas kernels  4.74 us (6%)
  local copies, waits for them, and re-layouts  2.3 us (3%)
  other arithmetic  0.93 us (1%)
    all_to_all x3, blocking collectives, exchange(): return lax.all_to_all(x, axes, 0, 0, tiled=True)  56.1 us
    ppermute x2, starting transfers between devices, swap_cores(): return lax.ppermute(x, 'co', [(0, 1), (1, 0)])  15.8 us
    unnamed x15, local copies, waits for them, and re-layouts  2.3 us
    pallas_call x1, Pallas kernels, on_device(): pl.pallas_call(grads_kernel, out_shape=(shape((2 * IMG, CMID), bf16), sha...  2.11 us
  transfers between devices with their start and end apart: 2, of which 1 were waited for; matrix products, arithmetic and copies ran while one was open for 2% of the time, Pallas kernels for 1%

profile of v9, /device:TPU:1, one launch (start us, length us, event | category | flops | bytes accessed | tf_op | source)
XLA Modules:
  0.0 81.0 jit_solution(9785144997093072061)
XLA Ops:
  0.6 0.0 copy-start.5
  0.6 0.0 copy-start
  0.7 1.1 %copy.12.x_ref = bf16[2,14,14,384]{3,2,1,0:T(8,128)(2,1)S(1)} copy(bf16[2,14,14,384]{3,0,2,1:T(2,128)(2,1)} %param.7) | data formatting | bytes 602112 | tf_op args[0]
  1.8 0.0 copy-done.5
  1.8 0.2 copy-done
  2.0 2.1 %grads.1 = (bf16[512,384]{1,0:T(8,128)(2,1)S(1)}, bf16[64,7,4,128]{3,2,1,0:T(4,128)(2,1)S(1)}, bf16[64,7,4,128]{3,2,1,0:T(4,128)(2,1)S(1)}) custom-call(bf16[2,14,14,384]{3,2,1,0:T(8,128)(2,1)S(1)} %copy.12.x_ref, bf16[2,14,14,384]{3,2,1,0:T(8,128)(2,1)S(1)} %copy.13.cot_ref, bf16[384,1152]{1,0:T(8,128)(2,1)S(1)} %copy-done), custom_call_target="tpu_custom_call" | custom-call | tf_op jit(solution)/shard_map/grads/pallas_call | solution.py:236
  4.1 8.7 %collective-permute-start = (bf16[64,7,4,128]{3,2,1,0:T(4,128)(2,1)S(1)}, bf16[64,7,4,128]{3,2,1,0:T(4,128)(2,1)S(1)}, u32[]{:S(2)}, u32[]{:S(2)}) collective-permute-start(bf16[64,7,4,128]{3,2,1,0:T(4,128)(2,1)S(1)} %get-tuple-element.13), channel_id=1, source_target_pairs={{0,8},{8,0},{1,9},{9,1},{2,10},{10,2},{3,11},{11,3},{4,12},{12,4},... | collective-permute-start | bytes 1376264 | tf_op jit(solution)/shard_map/ppermute | solution.py:226
  12.9 1.0 %input_grad.1 = bf16[2,14,14,384]{3,2,1,0:T(8,128)(2,1)S(1)} custom-call(bf16[512,384]{1,0:T(8,128)(2,1)S(1)} %get-tuple-element.14.pg_ref, bf16[384,1152]{1,0:T(8,128)(2,1)S(1)} %copy-done), custom_call_target="tpu_custom_call" | custom-call | tf_op jit(solution)/shard_map/input_grad/pallas_call | solution.py:256
  13.9 0.4 collective-permute-done
  14.3 0.2 add_convert_fusion
  14.5 0.0 copy-start.1
  14.5 0.0 copy-start.2
  14.5 0.0 copy-start.3
  14.6 27.3 %all_to_all.15.part_ref = bf16[64,7,4,128]{3,2,1,0:T(4,128)(2,1)S(1)} all-to-all(bf16[64,7,4,128]{3,2,1,0:T(4,128)(2,1)S(1)} %add_convert_fusion), channel_id=1, replica_groups=mesh['z'=8,'yh'=4,'co'=2,'yl'=2,'x'=4] {'z','yh','yl'}, dimensions={0} | all-to-all | bytes 917504 | tf_op jit(solution)/shard_map/all_to_all | solution.py:230
  41.9 0.1 reduce.1
  42.0 0.0 copy-start.4
  42.0 8.5 %all_to_all.16.in_ref = f32[4,48,128]{2,1,0:T(8,128)S(1)} all-to-all(f32[4,48,128]{2,1,0:T(8,128)S(1)} %reduce.1), channel_id=1, replica_groups=mesh['z'=8,'yh'=4,'co'=2,'yl'=2,'x'=4] {'x'}, dimensions={0} | all-to-all | bytes 196608 | tf_op jit(solution)/shard_map/all_to_all | solution.py:230
  50.5 0.3 adam.1
  50.9 20.3 %all_to_all.17.own_ref = bf16[64,7,4,128]{3,2,1,0:T(4,128)(2,1)S(1)} all-to-all(bf16[64,7,4,128]{3,2,1,0:T(4,128)(2,1)S(1)} %get-tuple-element.18), channel_id=1, replica_groups=mesh['z'=8,'yh'=4,'co'=2,'yl'=2,'x'=4] {'z','yh','yl'}, dimensions={0} | all-to-all | bytes 917504 | tf_op jit(solution)/shard_map/all_to_all | solution.py:230
  71.2 7.0 %collective-permute-start.1 = (bf16[64,7,4,128]{3,2,1,0:T(4,128)(2,1)S(1)}, bf16[64,7,4,128]{3,2,1,0:T(4,128)(2,1)S(1)}, u32[]{:S(2)}, u32[]{:S(2)}) collective-permute-start(bf16[64,7,4,128]{3,2,1,0:T(4,128)(2,1)S(1)} %all_to_all.17.own_ref), channel_id=1, source_target_pairs={{0,8},{8,0},{1,9},{9,1},{2,10},{10,2},{3,11},{11,3},{4,12},{12,4},... | collective-permute-start | bytes 1376264 | tf_op jit(solution)/shard_map/ppermute | solution.py:226
  78.2 0.9 %copy.14 = bf16[2,14,14,384]{3,0,2,1:T(2,128)(2,1)} copy(bf16[2,14,14,384]{3,2,1,0:T(8,128)(2,1)S(1)} %input_grad.1) | data formatting | bytes 602112
  79.2 0.7 multiply_subtract_fusion
  79.8 0.0 collective-permute-done.1.got_ref
  79.8 1.2 %assemble.1 = bf16[384,1152]{1,0:T(8,128)(2,1)} custom-call(bf16[64,7,4,128]{3,2,1,0:T(4,128)(2,1)S(1)} %all_to_all.17.own_ref, bf16[64,7,4,128]{3,2,1,0:T(4,128)(2,1)S(1)} %collective-permute-done.1.got_ref), custom_call_target="tpu_custom_call" | custom-call | tf_op jit(solution)/shard_map/assemble/pallas_call | solution.py:294
  (5 shorter events, 0.1 us)
Async XLA Ops:
  0.6 1.1 %copy-start.5 = (bf16[2,14,14,384]{3,0,2,1:T(2,128)(2,1)S(1)}, bf16[2,14,14,384]{3,0,2,1:T(2,128)(2,1)}, u32[]{:S(2)}) copy-start(bf16[2,14,14,384]{3,0,2,1:T(2,128)(2,1)} %param.8) | copy-start | bytes 903172
  0.6 1.3 %copy-start = (bf16[384,1152]{1,0:T(8,128)(2,1)S(1)}, bf16[384,1152]{1,0:T(8,128)(2,1)}, u32[]{:S(2)}) copy-start(bf16[384,1152]{1,0:T(8,128)(2,1)} %k_ref.3) | copy-start | bytes 2654212
  4.1 10.2 %collective-permute-start = (bf16[64,7,4,128]{3,2,1,0:T(4,128)(2,1)S(1)}, bf16[64,7,4,128]{3,2,1,0:T(4,128)(2,1)S(1)}, u32[]{:S(2)}, u32[]{:S(2)}) collective-permute-start(bf16[64,7,4,128]{3,2,1,0:T(4,128)(2,1)S(1)} %get-tuple-element.13), channel_id=1, source_target_pairs={{0,8},{8,0},{1,9},{9,1},{2,10},{10,2},{3,11},{11,3},{4,12},{12,4},... | collective-permute-start | bytes 1376264 | tf_op jit(solution)/shard_map/ppermute | solution.py:226
  14.5 27.4 %copy-start.1 = (f32[864]{0:T(1024)S(1)}, f32[864]{0:T(1024)}, u32[]{:S(2)}) copy-start(f32[864]{0:T(1024)} %master_ref.1) | copy-start | bytes 10372
  14.5 27.4 %copy-start.2 = (f32[864]{0:T(1024)S(1)}, f32[864]{0:T(1024)}, u32[]{:S(2)}) copy-start(f32[864]{0:T(1024)} %mean_ref.1) | copy-start | bytes 10372
  14.5 27.3 %copy-start.3 = (f32[864]{0:T(1024)S(1)}, f32[864]{0:T(1024)}, u32[]{:S(2)}) copy-start(f32[864]{0:T(1024)} %square_ref.1) | copy-start | bytes 10372
  42.0 8.5 %copy-start.4 = (f32[384]{0:T(512)S(1)}, f32[384]{0:T(512)}, u32[]{:S(2)}) copy-start(f32[384]{0:T(512)} %param.10) | copy-start | bytes 4612
  71.2 8.7 %collective-permute-start.1 = (bf16[64,7,4,128]{3,2,1,0:T(4,128)(2,1)S(1)}, bf16[64,7,4,128]{3,2,1,0:T(4,128)(2,1)S(1)}, u32[]{:S(2)}, u32[]{:S(2)}) collective-permute-start(bf16[64,7,4,128]{3,2,1,0:T(4,128)(2,1)S(1)} %all_to_all.17.own_ref), channel_id=1, source_target_pairs={{0,8},{8,0},{1,9},{9,1},{2,10},{10,2},{3,11},{11,3},{4,12},{12,4},... | collective-permute-start | bytes 1376264 | tf_op jit(solution)/shard_map/ppermute | solution.py:226
